TPU v7x, 256 devices: a whole 4x4x8 slice. The times are simulated.
256 devices in a mesh: pencil: 64 (over z, y_lo, x), lev: 4 (over y_hi, core).
Axes of the slice: x: 4, y: 4 (y_hi: 2, y_lo: 2; y = y_hi * 2 + y_lo), z: 8, core: 2. Of those that a mesh axis runs over, the one named last changes fastest.
Arguments:
- increment: bfloat16 [4, 4, 4096, 2048], P(None, 'lev', 'pencil'), may hold values from -6 to 6
- vert_coef: float32 [4, 4, 3], replicated, may hold values from -3 to 3
- latitude_block_matrix: bfloat16 [8, 5, 128, 128], replicated, may hold values from -0.25 to 0.25
- lat_band: int32 [16], replicated, may hold values from 0 to 7
- lat_offsets: int32 [5], replicated, may hold values from -3 to 3, as said below
- lon_blocks: bfloat16 [5, 128, 128], replicated, may hold values from -0.25 to 0.25
- lon_offsets: int32 [5], replicated, may hold values from -3 to 3, as said below
Outputs:
- filtered: float32 [2048, 4, 4, 4096], P('pencil', None, 'lev')
Inputs may be any that keep to these rules, and one draw needn't show every extreme that they name: `lat_offsets`: 5 distinct offsets, -3 and 3 always among them. `lon_offsets`: 5 distinct offsets, -3 and 3 always among them.
All inputs are finite; a program needn't handle non-finite values.
Results may differ from a plain program's by a relative error of at most 0.0041.
Values may be sent and summed in bfloat16 or wider, within the bound.
No kernel may reach another device: no remote copies, remote signals or barrier semaphores. Data moves between devices by JAX's collectives and lax.ppermute only.
A program may use at most 64 MiB of HBM per device.

v0:
```python
import jax
import jax.numpy as jnp
from jax import lax
from jax.sharding import PartitionSpec as P


def passed_along(value, axis, steps):
    count = lax.axis_size(axis)
    initial, last = (max(0, -steps), min(count, count - steps))
    return lax.ppermute(value, axis, [(source, source + steps) for source in range(initial, last)])


def latitude_weight_rows(latitude_block_matrix, lat_band, lat_offsets):
    count = lat_band.shape[0]
    block_ids = jnp.arange(count, dtype=jnp.int32)[:, None] - lat_offsets[None, :]
    clipped = jnp.clip(block_ids, 0, count - 1)
    shifted = lat_band[clipped]
    selector_matrix = (
        shifted[:, :, None]
        == jnp.arange(latitude_block_matrix.shape[0], dtype=jnp.int32)[None, None, :]
    ).astype(jnp.float32)
    table = jnp.einsum("skb,bkij->skij", selector_matrix, latitude_block_matrix.astype(jnp.float32))
    return table.reshape(count, -1, latitude_block_matrix.shape[-1]).astype(jnp.bfloat16)


def lat_apply(flat_rows, weight_matrix, offsets):
    size = weight_matrix.shape[-1]
    rows, nlat = flat_rows.shape
    nblk = nlat // size
    padded = jnp.pad(flat_rows, ((0, 0), (3 * size, 3 * size)))
    pieces = [
        lax.dynamic_slice_in_dim(padded, (3 - offsets[k]) * size, nlat, axis=1).reshape(
            rows, nblk, size
        )
        for k in range(offsets.shape[0])
    ]
    collected_rows = jnp.concatenate(pieces, axis=-1)
    adjoint_output = jnp.einsum(
        "eod,odv->ove", collected_rows, weight_matrix, preferred_element_type=jnp.float32
    )
    return adjoint_output.reshape(nlat, rows)


def lon_apply(block_in, blocks, offsets):
    size = blocks.shape[-1]
    width = block_in.shape[-1]
    nblk = width // size
    rolled = [
        jnp.roll(block_in, offsets[k] * size, axis=-1).reshape(block_in.shape[:-1] + (nblk, size))
        for k in range(blocks.shape[0])
    ]
    stacked = jnp.concatenate(rolled, axis=-1)
    adjoint_output = jnp.einsum(
        "...sq,qc->...sc", stacked, blocks.reshape(-1, size), preferred_element_type=jnp.float32
    )
    return adjoint_output.reshape(block_in.shape)


def per_device(
    increment, vert_coef, latitude_block_matrix, lat_band, lat_offsets, lon_blocks, lon_offsets
):
    variables = increment.shape[0]
    levels = increment.shape[1]
    nlat = increment.shape[3]
    own_index = lax.axis_index("lev")
    padded_coef = jnp.pad(vert_coef, ((0, 0), (1, 1), (0, 0)))
    own_coef = lax.dynamic_slice_in_dim(padded_coef, own_index * levels, levels + 2, axis=1)
    values = increment.astype(jnp.float32)
    level_terms = [
        own_coef[:, 1 : levels + 1, lag + 1][:, :, None, None] * values for lag in (-1, 0, 1)
    ]
    spread = jnp.pad(level_terms[0], ((0, 0), (0, 2), (0, 0), (0, 0)))
    spread = spread + jnp.pad(level_terms[1], ((0, 0), (1, 1), (0, 0), (0, 0)))
    spread = spread + jnp.pad(level_terms[2], ((0, 0), (2, 0), (0, 0), (0, 0)))
    from_above = passed_along(spread[:, :1], "lev", -1)
    from_below = passed_along(spread[:, levels + 1 :], "lev", 1)
    vertical = spread[:, 1 : levels + 1]
    vertical = vertical + from_below
    vertical = vertical + from_above
    vertical = vertical.astype(jnp.bfloat16)
    weight_matrix = latitude_weight_rows(latitude_block_matrix, lat_band, lat_offsets)

    def single_latitude(var_index):
        flat_rows = vertical[var_index].reshape(-1, nlat)
        adjoint_output = lat_apply(flat_rows, weight_matrix, lat_offsets)
        return adjoint_output.astype(jnp.bfloat16).reshape(nlat, levels, -1)

    lat_filtered = jnp.stack([single_latitude(var_index) for var_index in range(variables)], axis=1)
    result = lon_apply(
        lax.all_to_all(lat_filtered, "pencil", split_axis=0, concat_axis=3, tiled=True),
        blocks=lon_blocks,
        offsets=lon_offsets,
    )
    return result


def solution(mesh):
    in_specs = (P(None, "lev", "pencil", None), P(), P(), P(), P(), P(), P())
    out_specs = P("pencil", None, "lev", None)
    return jax.shard_map(
        per_device, mesh=mesh, in_specs=in_specs, out_specs=out_specs, check_vma=False
    )
```

profile of v0, /device:TPU:1, one launch (start us, length us, event | category | flops | bytes accessed | tf_op | source)
XLA Modules:
  0.0 105.7 jit_solution(1944680460779694993)
XLA Ops:
  0.0 1.0 fusion.50
  1.0 2.1 %convert_multiply_fusion.2 = (f32[4,1,64,2048]{3,2,1,0:T(8,128)S(1)}, f32[4,1,64,2048]{3,2,1,0:T(8,128)S(1)}, f32[4,1,64,2048]{3,2,1,0:T(8,128)S(1)}) fusion(bf16[4,1,64,2048]{3,2,1,0:T(8,128)(2,1)} %param.9, f32[4]{0:T(128)S(1)} %get-tuple-element.6, f32[4]{0:T(128)S(1)} %get-tuple-element.8, f32[4]{0:T(128)S(1)} %get-tuple-element.7), kind=kLoop, calls=%fused_computation.7 | loop fusion | flops 2097152 | bytes 7340080 | tf_op jit(solution)/shard_map/mul | solution.py:70
  3.1 0.8 pad_add_fusion
  3.9 2.7 %fusion.52 = (f32[4,1,64,2048]{3,2,1,0:T(8,128)}, f32[4,1,64,2048]{3,2,1,0:T(8,128)}) fusion(f32[4,3,64,2048]{3,2,1,0:T(8,128)S(1)} %pad_add_fusion), kind=kLoop, calls=%fused_computation.113 | loop fusion | bytes 8388608 | tf_op jit(solution)/shard_map/slice | solution.py:76
  6.6 1.4 %copy-done.3 = f32[4,3,64,2048]{3,2,1,0:T(8,128)} copy-done((f32[4,3,64,2048]{3,2,1,0:T(8,128)}, f32[4,3,64,2048]{3,2,1,0:T(8,128)S(1)}, u32[]{:S(2)}) %copy-start.3) | copy-done | bytes 6291480
  8.0 6.3 %collective-permute-start = (f32[4,1,64,2048]{3,2,1,0:T(8,128)}, f32[4,1,64,2048]{3,2,1,0:T(8,128)S(1)}, u32[]{:S(2)}, u32[]{:S(2)}) collective-permute-start(f32[4,1,64,2048]{3,2,1,0:T(8,128)} %get-tuple-element.9), channel_id=1, source_target_pairs={{0,1},{1,2},{2,3},{4,5},{5,6},{6,7},{8,9},{9,10},{10,11},{12,13},{... | collective-permute-start | bytes 6291464 | tf_op jit(solution)/shard_map/ppermute | solution.py:10
  14.3 1.9 %collective-permute-start.1 = (f32[4,1,64,2048]{3,2,1,0:T(8,128)}, f32[4,1,64,2048]{3,2,1,0:T(8,128)}, u32[]{:S(2)}, u32[]{:S(2)}) collective-permute-start(f32[4,1,64,2048]{3,2,1,0:T(8,128)} %get-tuple-element.10), channel_id=1, source_target_pairs={{1,0},{2,1},{3,2},{5,4},{6,5},{7,6},{9,8},{10,9},{11,10},{13,12},{... | collective-permute-start | bytes 6291464 | tf_op jit(solution)/shard_map/ppermute | solution.py:10
  16.3 0.7 fusion.54
  20.1 1.2 %gather_fusion = s32[80]{0:T(128)S(1)} fusion(s32[16]{0:T(128)S(1)} %copy-done.2, s32[1024]{0:T(1024)S(1)} %pad_clamp_fusion), kind=kCustom, calls=%fused_computation | custom fusion | bytes 960 | tf_op jit(solution)/shard_map/gather | solution.py:17
  21.5 3.5 %convolution_convert_fusion = bf16[5,16,128,128]{3,1,2,0:T(8,128)(2,1)S(1)} fusion(bf16[8,5,128,128]{3,2,1,0:T(8,128)(2,1)S(1)} %copy-done, s32[16,5]{0,1:T(8,128)S(1)} %copy.124), kind=kOutput, calls=%fused_computation.11 | convolution fusion | flops 22282880 | bytes 3932480 | tf_op jit(solution)/shard_map/skb,bkij->skij/dot_general | solution.py:22
  25.0 12.6 %collective-permute-done = f32[4,1,64,2048]{3,2,1,0:T(8,128)S(1)} collective-permute-done((f32[4,1,64,2048]{3,2,1,0:T(8,128)}, f32[4,1,64,2048]{3,2,1,0:T(8,128)S(1)}, u32[]{:S(2)}, u32[]{:S(2)}) %collective-permute-start) | collective-permute-done | bytes 2097184 | tf_op jit(solution)/shard_map/ppermute | solution.py:10
  37.6 5.9 %collective-permute-done.1 = f32[4,1,64,2048]{3,2,1,0:T(8,128)} collective-permute-done((f32[4,1,64,2048]{3,2,1,0:T(8,128)}, f32[4,1,64,2048]{3,2,1,0:T(8,128)}, u32[]{:S(2)}, u32[]{:S(2)}) %collective-permute-start.1) | collective-permute-done | bytes 2097184 | tf_op jit(solution)/shard_map/ppermute | solution.py:10
  43.5 2.7 %fusion.4 = bf16[4,1,64,2048]{3,2,1,0:T(8,128)(2,1)S(1)} fusion(f32[4,1,64,2048]{3,2,1,0:T(8,128)} %collective-permute-done.1, f32[4,1,64,2048]{3,2,1,0:T(8,128)S(1)} %collective-permute-done, f32[4,3,64,2048]{3,2,1,0:T(8,128)} %copy-done.3), kind=kLoop, calls=%fused_computation.10 | loop fusion | flops 1572864 | bytes 7340032 | tf_op jit(solution)/shard_map/convert_element_type | solution.py:80
  46.3 0.4 fusion.30
  47.3 1.2 %fusion.23 = bf16[16,128,64]{1,2,0:T(8,128)(2,1)S(1)} fusion(bf16[64,16,640]{2,0,1:T(8,128)(2,1)S(1)} %bitcast_dynamic-update-slice_fusion.15, bf16[16,640,128]{2,0,1:T(8,128)(2,1)S(1)} %bitcast.187), kind=kOutput, calls=%fused_computation.24 | convolution fusion | flops 167903232 | bytes 4194304 | tf_op jit(solution)/shard_map/eod,odv->ove/dot_general | solution.py:38
  48.5 0.2 copy.132
  49.3 1.2 %copy-done.5 = bf16[5,16,128,128]{3,1,2,0:T(8,128)(2,1)S(1)} copy-done((bf16[5,16,128,128]{3,1,2,0:T(8,128)(2,1)S(1)}, bf16[5,16,128,128]{3,1,2,0:T(8,128)(2,1)}, u32[]{:S(2)}) %copy-start.5) | copy-done | bytes 2621464
  50.5 1.2 %fusion.20 = bf16[16,128,64]{1,2,0:T(8,128)(2,1)S(1)} fusion(bf16[64,16,640]{2,0,1:T(8,128)(2,1)S(1)} %bitcast_dynamic-update-slice_fusion.10, bf16[16,640,128]{2,0,1:T(8,128)(2,1)S(1)} %bitcast.189), kind=kOutput, calls=%fused_computation.23 | convolution fusion | flops 167903232 | bytes 4194304 | tf_op jit(solution)/shard_map/eod,odv->ove/dot_general | solution.py:38
  51.7 0.2 copy.139
  52.0 0.4 fusion.40
  53.0 1.2 %copy-done.6 = bf16[5,16,128,128]{3,1,2,0:T(8,128)(2,1)S(1)} copy-done((bf16[5,16,128,128]{3,1,2,0:T(8,128)(2,1)S(1)}, bf16[5,16,128,128]{3,1,2,0:T(8,128)(2,1)}, u32[]{:S(2)}) %copy-start.6) | copy-done | bytes 2621464
  54.2 1.2 %fusion.17 = bf16[16,128,64]{1,2,0:T(8,128)(2,1)S(1)} fusion(bf16[64,16,640]{2,0,1:T(8,128)(2,1)S(1)} %bitcast_dynamic-update-slice_fusion.5, bf16[16,640,128]{2,0,1:T(8,128)(2,1)S(1)} %bitcast.190), kind=kOutput, calls=%fused_computation.22 | convolution fusion | flops 167903232 | bytes 4194304 | tf_op jit(solution)/shard_map/eod,odv->ove/dot_general | solution.py:38
  55.4 0.2 copy.146
  56.2 2.9 %fusion.14 = bf16[16,128,64]{1,2,0:T(8,128)(2,1)S(1)} fusion(bf16[64,16,640]{2,0,1:T(8,128)(2,1)S(1)} %bitcast_dynamic-update-slice_fusion, bf16[16,640,128]{2,0,1:T(8,128)(2,1)} %bitcast.188), kind=kOutput, calls=%fused_computation.21 | convolution fusion | flops 167903232 | bytes 4194304 | tf_op jit(solution)/shard_map/eod,odv->ove/dot_general | solution.py:38
  59.2 0.2 copy.153
  59.5 0.1 pad_maximum_fusion
  59.6 1.4 %copy.154 = bf16[2048,4,1,64]{3,1,2,0:T(4,128)(2,1)S(1)} copy(bf16[2048,4,1,64]{0,3,2,1:T(8,128)(2,1)S(1)} %pad_maximum_fusion) | data formatting | bytes 2097152 | tf_op jit(solution)/shard_map/stack | solution.py:88
  61.0 2.5 %reshape.263 = bf16[64,2,4096]{2,1,0:T(2,128)(2,1)} reshape(bf16[2048,1,4,64]{3,2,1,0:T(4,128)(2,1)S(1)} %bitcast.174) | data formatting | bytes 2097152
  63.5 11.8 %all-to-all-start = ((bf16[64,2,4096]{2,1,0:T(2,128)(2,1)}), bf16[64,2,4096]{2,1,0:T(2,128)(2,1)S(1)}, u32[]{:S(2)}, u32[]{:S(2)}) async-start(bf16[64,2,4096]{2,1,0:T(2,128)(2,1)} %reshape.263), calls=%async_computation | async-start | bytes 2097152 | tf_op jit(solution)/shard_map/all_to_all | solution.py:90
  75.3 0.7 fusion.53
  79.2 13.4 %all-to-all-done = bf16[64,2,4096]{2,1,0:T(2,128)(2,1)S(1)} async-done(((bf16[64,2,4096]{2,1,0:T(2,128)(2,1)}), bf16[64,2,4096]{2,1,0:T(2,128)(2,1)S(1)}, u32[]{:S(2)}, u32[]{:S(2)}) %all-to-all-start) | async-done | bytes 1048608 | tf_op jit(solution)/shard_map/all_to_all | solution.py:90
  92.6 1.3 %reshape.264 = bf16[2048,1,4,64]{3,2,1,0:T(4,128)(2,1)S(1)} reshape(bf16[64,2,4096]{2,1,0:T(2,128)(2,1)S(1)} %all-to-all-done) | data formatting | bytes 2097152
  93.9 0.3 copy.155
  94.2 0.8 copy.156
  95.0 1.7 %all_to_all.16 = bf16[32,4,1,4096]{3,0,1,2:T(8,128)(2,1)S(1)} reshape(bf16[32,4,1,64,64]{4,3,0,1,2:T(8,128)(2,1)S(1)} %copy.156) | data formatting | bytes 2097152 | tf_op jit(solution)/shard_map/all_to_all | solution.py:90
  96.9 3.0 %constant_dynamic-slice_fusion.2 = (bf16[32,4,1,4096]{3,0,1,2:T(8,128)(2,1)S(1)}, bf16[32,4,1,4096]{3,0,1,2:T(8,128)(2,1)S(1)}, bf16[32,4,1,4096]{3,0,1,2:T(8,12...) fusion(bf16[32,4,1,8192]{3,0,1,2:T(8,128)(2,1)S(1)} %constant_dynamic-update-slice_fusion, ...), kind=kLoop, calls=%fused_computation.103 | loop fusion | bytes 10485780 | tf_op jit(solution)/shard_map/jit(_roll_dynamic)/dynamic_slice | solution.py:49
  99.9 0.2 copy.191
  100.1 0.2 constant_dynamic-update-slice_fusion.6
  100.3 0.2 copy.192
  100.6 0.2 copy.193
  100.8 0.2 copy.194
  101.1 0.2 copy.195
  101.3 0.3 constant_dynamic-update-slice_fusion.5
  101.6 0.3 constant_dynamic-update-slice_fusion.4
  101.9 0.3 constant_dynamic-update-slice_fusion.3
  102.2 0.3 constant_dynamic-update-slice_fusion.2
  102.4 0.4 copy-done.9
  102.8 2.9 %fusion = f32[32,4,32,128]{3,2,1,0:T(8,128)} fusion(bf16[640,128,1,1]{1,0,3,2:T(8,128)(2,1)S(1)} %bitcast.191, bf16[32,4,1,32,640]{4,3,0,1,2:T(8,128)(2,1)S(1)} %constant_dynamic-update-slice_fusion.2), kind=kOutput, calls=%fused_computation.2 | convolution fusion | flops 671088640 | bytes 7503872 | tf_op jit(solution)/shard_map/...sq,qc->...sc/dot_general | solution.py:53
  (48 shorter events, 3.0 us)
Async XLA Ops:
  0.0 21.5 %copy-start = (bf16[8,5,128,128]{3,2,1,0:T(8,128)(2,1)S(1)}, bf16[8,5,128,128]{3,2,1,0:T(8,128)(2,1)}, u32[]{:S(2)}) copy-start(bf16[8,5,128,128]{3,2,1,0:T(8,128)(2,1)} %param.11) | copy-start | bytes 3932164
  3.9 4.1 %copy-start.3 = (f32[4,3,64,2048]{3,2,1,0:T(8,128)}, f32[4,3,64,2048]{3,2,1,0:T(8,128)S(1)}, u32[]{:S(2)}) copy-start(f32[4,3,64,2048]{3,2,1,0:T(8,128)S(1)} %pad_add_fusion) | copy-start | bytes 18874372
  3.9 12.3 %copy-start.7 = (s32[5]{0:T(128)S(1)}, s32[5]{0:T(128)}, u32[]{:S(2)}) copy-start(s32[5]{0:T(128)} %param.13) | copy-start | bytes 64
  8.0 12.1 %copy-start.2 = (s32[16]{0:T(128)S(1)}, s32[16]{0:T(128)}, u32[]{:S(2)}) copy-start(s32[16]{0:T(128)} %param.12) | copy-start | bytes 196
  8.0 29.6 %collective-permute-start = (f32[4,1,64,2048]{3,2,1,0:T(8,128)}, f32[4,1,64,2048]{3,2,1,0:T(8,128)S(1)}, u32[]{:S(2)}, u32[]{:S(2)}) collective-permute-start(f32[4,1,64,2048]{3,2,1,0:T(8,128)} %get-tuple-element.9), channel_id=1, source_target_pairs={{0,1},{1,2},{2,3},{4,5},{5,6},{6,7},{8,9},{9,10},{10,11},{12,13},{... | collective-permute-start | bytes 6291464 | tf_op jit(solution)/shard_map/ppermute | solution.py:10
  14.3 29.2 %collective-permute-start.1 = (f32[4,1,64,2048]{3,2,1,0:T(8,128)}, f32[4,1,64,2048]{3,2,1,0:T(8,128)}, u32[]{:S(2)}, u32[]{:S(2)}) collective-permute-start(f32[4,1,64,2048]{3,2,1,0:T(8,128)} %get-tuple-element.10), channel_id=1, source_target_pairs={{1,0},{2,1},{3,2},{5,4},{6,5},{7,6},{9,8},{10,9},{11,10},{13,12},{... | collective-permute-start | bytes 6291464 | tf_op jit(solution)/shard_map/ppermute | solution.py:10
  25.0 22.3 %copy-start.4 = (bf16[5,16,128,128]{3,1,2,0:T(8,128)(2,1)}, bf16[5,16,128,128]{3,1,2,0:T(8,128)(2,1)S(1)}, u32[]{:S(2)}) copy-start(bf16[5,16,128,128]{3,1,2,0:T(8,128)(2,1)S(1)} %convolution_convert_fusion) | copy-start | bytes 7864324
  48.8 1.7 %copy-start.5 = (bf16[5,16,128,128]{3,1,2,0:T(8,128)(2,1)S(1)}, bf16[5,16,128,128]{3,1,2,0:T(8,128)(2,1)}, u32[]{:S(2)}) copy-start(bf16[5,16,128,128]{3,1,2,0:T(8,128)(2,1)} %copy-done.4) | copy-start | bytes 7864324
  52.5 1.7 %copy-start.6 = (bf16[5,16,128,128]{3,1,2,0:T(8,128)(2,1)S(1)}, bf16[5,16,128,128]{3,1,2,0:T(8,128)(2,1)}, u32[]{:S(2)}) copy-start(bf16[5,16,128,128]{3,1,2,0:T(8,128)(2,1)} %copy-done.4) | copy-start | bytes 7864324
  61.0 14.3 %copy-start.8 = (s32[5]{0:T(128)S(1)}, s32[5]{0:T(128)}, u32[]{:S(2)}) copy-start(s32[5]{0:T(128)} %param.15) | copy-start | bytes 64
  63.5 29.1 %all-to-all-start = ((bf16[64,2,4096]{2,1,0:T(2,128)(2,1)}), bf16[64,2,4096]{2,1,0:T(2,128)(2,1)S(1)}, u32[]{:S(2)}, u32[]{:S(2)}) async-start(bf16[64,2,4096]{2,1,0:T(2,128)(2,1)} %reshape.263), calls=%async_computation | async-start | bytes 2097152 | tf_op jit(solution)/shard_map/all_to_all | solution.py:90
  101.9 0.9 copy-start.9
  102.4 3.3 %copy-start.1 = (bf16[8,5,128,128]{3,2,1,0:T(8,128)(2,1)S(1)}, bf16[8,5,128,128]{3,2,1,0:T(8,128)(2,1)}, u32[]{:S(2)}) copy-start(bf16[8,5,128,128]{3,2,1,0:T(8,128)(2,1)} %param.11) | copy-start | bytes 3932164
where the time goes:
time: 106 us
  waiting for transfers between devices  31.9 us (30%)
  local copies, waits for them, and re-layouts  28.3 us (27%)
  starting transfers between devices  20 us (19%)
  matrix products  12.8 us (12%)
  between operations  6.86 us (6%)
  other arithmetic  5.74 us (5%)
    ppermute x2, waiting for transfers between devices, passed_along(): lax.ppermute(value, axis, [(source, source + steps) for source in range(i...  18.5 us
    all_to_all x1, waiting for transfers between devices, per_device(): lax.all_to_all(lat_filtered, 'pencil', split_axis=0, concat_axis=3, tiled...  13.4 us
    unnamed x50, local copies, waits for them, and re-layouts  12.7 us
    all_to_all x1, starting transfers between devices, per_device(): lax.all_to_all(lat_filtered, 'pencil', split_axis=0, concat_axis=3, tiled...  11.8 us
    ppermute x2, starting transfers between devices, passed_along(): lax.ppermute(value, axis, [(source, source + steps) for source in range(i...  8.25 us
    dot_general x4, matrix products, lat_apply(): jnp.einsum('eod,odv->ove', collected_rows, weight_matrix, preferred_eleme...  6.45 us
    dot_general x1, matrix products, latitude_weight_rows(): jnp.einsum('skb,bkij->skij', selector_matrix, latitude_block_matrix.astyp...  3.51 us
    dynamic_slice x1, local copies, waits for them, and re-layouts, lon_apply(): jnp.roll(block_in, offsets[k] * size, axis=-1)  3 us
  transfers between devices with their start and end apart: 3, of which 3 were waited for; matrix products, arithmetic and copies ran while one was open for 6% of the time, Pallas kernels for 0%

commit v1 on v0

v1 whole, which is shorter than its diff:
```python
import jax
import jax.numpy as jnp
from jax import lax
from jax.experimental import pallas as pl
from jax.experimental.pallas import tpu as pltpu
from jax.sharding import PartitionSpec as P

BLK = 128
REACH = 3


def lat_kernel(nblk, coef, band, offs, lev, own, below, above, table, out, blocks):
    variables, _, rows, _ = own.shape
    levels = coef.shape[1]
    taps = offs.shape[0]
    level = lev[0]
    lower = jnp.maximum(level - 1, 0)
    upper = jnp.minimum(level + 1, levels - 1)
    zeros = jnp.zeros(blocks.shape[1:], blocks.dtype)
    for edge in range(REACH):
        blocks[edge] = zeros
        blocks[REACH + nblk + edge] = zeros
    for v in range(variables):
        c_below = jnp.where(level > 0, coef[v, lower, 2], 0.0)
        c_own = coef[v, level, 1]
        c_above = jnp.where(level < levels - 1, coef[v, upper, 0], 0.0)
        for t in range(nblk):
            cols = slice(t * BLK, (t + 1) * BLK)
            total = c_below * below[v, 0, :, cols].astype(jnp.float32)
            total = total + c_own * own[v, 0, :, cols].astype(jnp.float32)
            total = total + c_above * above[v, 0, :, cols].astype(jnp.float32)
            blocks[REACH + t, v * rows : (v + 1) * rows, :] = total.astype(blocks.dtype)
    for s in range(nblk):
        lhs, rhs = [], []
        for k in range(taps):
            source = s - offs[k]
            lhs.append(blocks[source + REACH])
            rhs.append(table[band[jnp.clip(source, 0, nblk - 1)], k])
        total = jnp.dot(
            jnp.concatenate(lhs, axis=1),
            jnp.concatenate(rhs, axis=0),
            preferred_element_type=jnp.float32,
        )
        out[s * BLK : (s + 1) * BLK, :] = total.T.astype(out.dtype)


def lon_kernel(offs, data, weights, out, blocks):
    peers, lats, width = data.shape
    variables = width // (BLK // 2)
    nblk = peers // 2
    taps = offs.shape[0]
    group = 8
    half = BLK // 2
    first = lax.broadcasted_iota(jnp.int32, (lats, BLK), 1) < half
    for t in range(nblk):
        for pair in range(variables // 2):
            cols = slice(pair * BLK, (pair + 1) * BLK)
            a = data[2 * t, :, cols].astype(jnp.float32)
            b = data[2 * t + 1, :, cols].astype(jnp.float32)
            even = jnp.where(first, a, pltpu.roll(b, half, 1))
            odd = jnp.where(first, pltpu.roll(a, half, 1), b)
            v = 2 * pair
            blocks[t, v * lats : (v + 1) * lats, :] = even.astype(blocks.dtype)
            blocks[t, (v + 1) * lats : (v + 2) * lats, :] = odd.astype(blocks.dtype)
    rhs = jnp.concatenate([weights[k] for k in range(taps)], axis=0)
    for g in range(0, nblk, group):
        lhs = []
        for s in range(g, g + group):
            lhs.append(
                jnp.concatenate(
                    [blocks[lax.rem(s - offs[k] + nblk, nblk)] for k in range(taps)], axis=1
                )
            )
        total = jnp.dot(
            jnp.concatenate(lhs, axis=0), rhs, preferred_element_type=jnp.float32
        )
        for n, s in enumerate(range(g, g + group)):
            for v in range(variables):
                row = (n * variables + v) * lats
                out[pl.ds(v * nblk + s, lats, stride=variables * nblk), :] = total[
                    row : row + lats
                ]


def per_device(
    increment, vert_coef, latitude_block_matrix, lat_band, lat_offsets, lon_blocks, lon_offsets
):
    variables, _, rows, nlat = increment.shape
    nblk = nlat // BLK
    npencil = lax.axis_size("pencil")
    nlev = lax.axis_size("lev")
    nlon = rows * npencil
    lats = nlat // npencil
    smem = pl.BlockSpec(memory_space=pltpu.SMEM)
    vmem = pl.BlockSpec(memory_space=pltpu.VMEM)

    below = lax.ppermute(increment, "lev", [(n, n + 1) for n in range(nlev - 1)])
    above = lax.ppermute(increment, "lev", [(n + 1, n) for n in range(nlev - 1)])
    own_level = lax.axis_index("lev").astype(jnp.int32).reshape(1)

    filtered = pl.pallas_call(
        lambda *refs: lat_kernel(nblk, *refs),
        out_shape=jax.ShapeDtypeStruct((nlat, variables * rows), jnp.bfloat16),
        in_specs=[smem] * 4 + [vmem] * 4,
        out_specs=vmem,
        scratch_shapes=[pltpu.VMEM((nblk + 2 * REACH, variables * rows, BLK), jnp.bfloat16)],
        compiler_params=pltpu.CompilerParams(vmem_limit_bytes=40 * 2**20),
        name="vertical_and_latitude",
    )(vert_coef, lat_band, lat_offsets, own_level, increment, below, above, latitude_block_matrix)

    moved = lax.all_to_all(filtered, "pencil", split_axis=0, concat_axis=0, tiled=True)

    result = pl.pallas_call(
        lon_kernel,
        out_shape=jax.ShapeDtypeStruct((lats * variables * nlon // BLK, BLK), jnp.float32),
        in_specs=[smem, vmem, vmem],
        out_specs=vmem,
        scratch_shapes=[pltpu.VMEM((nlon // BLK, lats * variables, BLK), jnp.bfloat16)],
        compiler_params=pltpu.CompilerParams(vmem_limit_bytes=40 * 2**20),
        name="longitude",
    )(lon_offsets, moved.reshape(npencil, lats, variables * rows), lon_blocks)
    return result.reshape(lats, variables, 1, nlon)


def solution(mesh):
    in_specs = (P(None, "lev", "pencil", None), P(), P(), P(), P(), P(), P())
    out_specs = P("pencil", None, "lev", None)
    return jax.shard_map(
        per_device, mesh=mesh, in_specs=in_specs, out_specs=out_specs, check_vma=False
    )
```

time: 106 us -> 65.7 us (0.62)
  blocking collectives: 0 us -> 29.2 us
  local copies, waits for them, and re-layouts: 28.3 us -> 4.66 us
  waiting for transfers between devices: 31.9 us -> 15.1 us
  matrix products: 12.8 us -> 0 us
  starting transfers between devices: 20 us -> 8.13 us
  Pallas kernels: 0 us -> 8.23 us
  between operations: 6.86 us -> 0.05 us
  other arithmetic: 5.74 us -> 0 us
    all_to_all x0 -> x1, blocking collectives: none -> 29.2 us  [per_device(): lax.all_to_all(filtered, 'pencil', split_axis=0, concat_axis=0, tiled=True)]
    all_to_all x1 -> x0, waiting for transfers between devices: 13.4 us -> none  [per_device(): lax.all_to_all(lat_filtered, 'pencil', split_axis=0, concat_axis=3, tiled...]
    dot_general x6 -> x0, matrix products: 12.8 us -> none  [the longest x4 6.45 us: lat_apply(): jnp.einsum('eod,odv->ove', collected_rows, weight_matrix, preferred_eleme...]
    all_to_all x1 -> x0, starting transfers between devices: 11.8 us -> none  [per_device(): lax.all_to_all(lat_filtered, 'pencil', split_axis=0, concat_axis=3, tiled...]
    pallas_call x0 -> x2, Pallas kernels: none -> 8.23 us  [the longest x1 5.32 us: per_device(): pl.pallas_call(lon_kernel, out_shape=jax.ShapeDtypeStruct((lats * variabl...]
    unnamed x50 -> x13, local copies, waits for them, and re-layouts: 12.7 us -> 4.66 us
    slice x4 -> x0, local copies, waits for them, and re-layouts: 5.01 us -> none  [the longest x1 2.66 us: per_device(): from_below = passed_along(spread[:, levels + 1:], 'lev', 1)]
    ppermute x2, waiting for transfers between devices: 18.5 us -> 15.1 us  [the longest x1 9.31 us: per_device(): lax.ppermute(increment, 'lev', [(n, n + 1) for n in range(nlev - 1)])]
  transfers between devices with their start and end apart: 3 -> 2, of which waited for: 3 -> 2; matrix products, arithmetic and copies ran while one was open for 6% -> 1% of each run, Pallas kernels for 0% -> 0%
where the time goes in v1:
time: 65.7 us; the launch traced here: 65.4 us
  blocking collectives  29.2 us (44%)
  waiting for transfers between devices  15.1 us (23%)
  Pallas kernels  8.23 us (13%)
  starting transfers between devices  8.13 us (12%)
  local copies, waits for them, and re-layouts  4.66 us (7%)
    all_to_all x1, blocking collectives, per_device(): lax.all_to_all(filtered, 'pencil', split_axis=0, concat_axis=0, tiled=True)  29.2 us
    ppermute x1, waiting for transfers between devices, per_device(): lax.ppermute(increment, 'lev', [(n, n + 1) for n in range(nlev - 1)])  9.31 us
    ppermute x1, starting transfers between devices, per_device(): lax.ppermute(increment, 'lev', [(n, n + 1) for n in range(nlev - 1)])  6.2 us
    ppermute x1, waiting for transfers between devices, per_device(): lax.ppermute(increment, 'lev', [(n + 1, n) for n in range(nlev - 1)])  5.8 us
    pallas_call x1, Pallas kernels, per_device(): pl.pallas_call(lon_kernel, out_shape=jax.ShapeDtypeStruct((lats * variabl...  5.32 us
    unnamed x13, local copies, waits for them, and re-layouts  4.66 us
    pallas_call x1, Pallas kernels, per_device(): pl.pallas_call(lambda *refs: lat_kernel(nblk, *refs), out_shape=jax.Shape...  2.91 us
    ppermute x1, starting transfers between devices, per_device(): lax.ppermute(increment, 'lev', [(n + 1, n) for n in range(nlev - 1)])  1.92 us
  transfers between devices with their start and end apart: 2, of which 2 were waited for; matrix products, arithmetic and copies ran while one was open for 1% of the time, Pallas kernels for 0%

profile of v1, /device:TPU:1, one launch (start us, length us, event | category | flops | bytes accessed | tf_op | source)
XLA Modules:
  0.0 65.4 jit_solution(4121860994133276224)
XLA Ops:
  0.0 6.2 %collective-permute-start = (bf16[4,1,64,2048]{3,2,1,0:T(8,128)(2,1)}, bf16[4,1,64,2048]{3,2,1,0:T(8,128)(2,1)S(1)}, u32[]{:S(2)}, u32[]{:S(2)}) collective-permute-start(bf16[4,1,64,2048]{3,2,1,0:T(8,128)(2,1)} %refs_4_.1), channel_id=1, source_target_pairs={{0,1},{1,2},{2,3},{4,5},{5,6},{6,7},{8,9},{9,10},{10,11},{12,13},{... | collective-permute-start | bytes 3145736 | tf_op jit(solution)/shard_map/ppermute | solution.py:97
  6.2 1.9 %collective-permute-start.1 = (bf16[4,1,64,2048]{3,2,1,0:T(8,128)(2,1)}, bf16[4,1,64,2048]{3,2,1,0:T(8,128)(2,1)S(1)}, u32[]{:S(2)}, u32[]{:S(2)}) collective-permute-start(bf16[4,1,64,2048]{3,2,1,0:T(8,128)(2,1)} %refs_4_.1), channel_id=1, source_target_pairs={{1,0},{2,1},{3,2},{5,4},{6,5},{7,6},{9,8},{10,9},{11,10},{13,12},{... | collective-permute-start | bytes 3145736 | tf_op jit(solution)/shard_map/ppermute | solution.py:98
  8.1 0.8 %copy.8.refs_0_ = f32[4,4,3]{2,1,0:T(4,128)S(1)} copy(f32[4,4,3]{1,0,2:T(4,128)} %param.8) | data formatting | bytes 384 | tf_op args[1]
  8.9 9.3 %collective-permute-done.refs_5_ = bf16[4,1,64,2048]{3,2,1,0:T(8,128)(2,1)S(1)} collective-permute-done((bf16[4,1,64,2048]{3,2,1,0:T(8,128)(2,1)}, bf16[4,1,64,2048]{3,2,1,0:T(8,128)(2,1)S(1)}, u32[]{:S(2)}, u32[]{:S(2)}) %collective-permute-start) | collective-permute-done | bytes 1048608 | tf_op jit(solution)/shard_map/ppermute | solution.py:97
  18.2 5.8 %collective-permute-done.1.refs_6_ = bf16[4,1,64,2048]{3,2,1,0:T(8,128)(2,1)S(1)} collective-permute-done((bf16[4,1,64,2048]{3,2,1,0:T(8,128)(2,1)}, bf16[4,1,64,2048]{3,2,1,0:T(8,128)(2,1)S(1)}, u32[]{:S(2)}, u32[]{:S(2)}) %collective-permute-start.1) | collective-permute-done | bytes 1048608 | tf_op jit(solution)/shard_map/ppermute | solution.py:98
  24.0 0.0 copy-start
  24.0 1.3 %copy-done = bf16[8,5,128,128]{3,2,1,0:T(8,128)(2,1)S(1)} copy-done((bf16[8,5,128,128]{3,2,1,0:T(8,128)(2,1)S(1)}, bf16[8,5,128,128]{3,2,1,0:T(8,128)(2,1)}, u32[]{:S(2)}) %copy-start) | copy-done | bytes 1310744
  25.4 0.0 copy-start.1
  25.4 1.2 %copy-done.1 = bf16[4,1,64,2048]{3,2,1,0:T(8,128)(2,1)S(1)} copy-done((bf16[4,1,64,2048]{3,2,1,0:T(8,128)(2,1)S(1)}, bf16[4,1,64,2048]{3,2,1,0:T(8,128)(2,1)}, u32[]{:S(2)}) %copy-start.1) | copy-done | bytes 1048600
  26.6 0.0 copy-start.3
  26.6 0.7 copy-done.3
  27.2 0.0 copy-start.4
  27.2 0.7 copy-done.4
  27.9 2.9 %vertical_and_latitude.1 = bf16[2048,256]{1,0:T(8,128)(2,1)S(1)} custom-call(f32[4,4,3]{2,1,0:T(4,128)S(1)} %copy.8.refs_0_, s32[16]{0:T(128)S(1)} %copy-done.3, s32[5]{0:T(128)S(1)} %copy-done.4, s32[1]{0:T(128)} %bitcast.refs_3_, bf16[4,1,64,2048]{3,2,1,0:T(8,128)(2,1)S(1)} %copy-done.1, bf16[4,1,64,2048]{3,2,1,0:T(8,128)(2,1)S(1)} %collective-permute-done.refs_5_, ...), custom_call_target="tpu_custom_call" | custom-call | tf_op jit(solution)/shard_map/vertical_and_latitude/pallas_call | solution.py:101
  30.8 0.0 copy-start.2
  30.8 0.0 copy-start.5
  30.8 29.2 %all_to_all.9.data = bf16[64,32,256]{2,1,0:T(8,128)(2,1)S(1)} all-to-all(bf16[64,32,256]{2,1,0:T(8,128)(2,1)S(1)} %bitcast.3), channel_id=1, replica_groups=mesh['pencil'=64,'lev'=4] {'pencil'}, dimensions={0} | all-to-all | bytes 2097152 | tf_op jit(solution)/shard_map/all_to_all | solution.py:111
  60.1 0.0 copy-done.2
  60.1 0.0 copy-done.5
  60.1 5.3 %longitude.1 = f32[4096,128]{1,0:T(8,128)} custom-call(s32[5]{0:T(128)S(1)} %copy-done.5, bf16[64,32,256]{2,1,0:T(8,128)(2,1)S(1)} %all_to_all.9.data, bf16[5,128,128]{2,1,0:T(8,128)(2,1)S(1)} %copy-done.2), custom_call_target="tpu_custom_call" | custom-call | tf_op jit(solution)/shard_map/longitude/pallas_call | solution.py:113
Async XLA Ops:
  0.0 18.2 %collective-permute-start = (bf16[4,1,64,2048]{3,2,1,0:T(8,128)(2,1)}, bf16[4,1,64,2048]{3,2,1,0:T(8,128)(2,1)S(1)}, u32[]{:S(2)}, u32[]{:S(2)}) collective-permute-start(bf16[4,1,64,2048]{3,2,1,0:T(8,128)(2,1)} %refs_4_.1), channel_id=1, source_target_pairs={{0,1},{1,2},{2,3},{4,5},{5,6},{6,7},{8,9},{9,10},{10,11},{12,13},{... | collective-permute-start | bytes 3145736 | tf_op jit(solution)/shard_map/ppermute | solution.py:97
  6.2 17.8 %collective-permute-start.1 = (bf16[4,1,64,2048]{3,2,1,0:T(8,128)(2,1)}, bf16[4,1,64,2048]{3,2,1,0:T(8,128)(2,1)S(1)}, u32[]{:S(2)}, u32[]{:S(2)}) collective-permute-start(bf16[4,1,64,2048]{3,2,1,0:T(8,128)(2,1)} %refs_4_.1), channel_id=1, source_target_pairs={{1,0},{2,1},{3,2},{5,4},{6,5},{7,6},{9,8},{10,9},{11,10},{13,12},{... | collective-permute-start | bytes 3145736 | tf_op jit(solution)/shard_map/ppermute | solution.py:98
  24.0 1.3 %copy-start = (bf16[8,5,128,128]{3,2,1,0:T(8,128)(2,1)S(1)}, bf16[8,5,128,128]{3,2,1,0:T(8,128)(2,1)}, u32[]{:S(2)}) copy-start(bf16[8,5,128,128]{3,2,1,0:T(8,128)(2,1)} %refs_7_.1) | copy-start | bytes 3932164
  25.4 1.2 %copy-start.1 = (bf16[4,1,64,2048]{3,2,1,0:T(8,128)(2,1)S(1)}, bf16[4,1,64,2048]{3,2,1,0:T(8,128)(2,1)}, u32[]{:S(2)}) copy-start(bf16[4,1,64,2048]{3,2,1,0:T(8,128)(2,1)} %refs_4_.1) | copy-start | bytes 3145732
  26.6 0.7 %copy-start.3 = (s32[16]{0:T(128)S(1)}, s32[16]{0:T(128)}, u32[]{:S(2)}) copy-start(s32[16]{0:T(128)} %refs_1_.1) | copy-start | bytes 196
  27.2 0.7 %copy-start.4 = (s32[5]{0:T(128)S(1)}, s32[5]{0:T(128)}, u32[]{:S(2)}) copy-start(s32[5]{0:T(128)} %refs_2_.1) | copy-start | bytes 64
  30.8 29.3 %copy-start.2 = (bf16[5,128,128]{2,1,0:T(8,128)(2,1)S(1)}, bf16[5,128,128]{2,1,0:T(8,128)(2,1)}, u32[]{:S(2)}) copy-start(bf16[5,128,128]{2,1,0:T(8,128)(2,1)} %weights.1) | copy-start | bytes 491524
  30.8 29.3 %copy-start.5 = (s32[5]{0:T(128)S(1)}, s32[5]{0:T(128)}, u32[]{:S(2)}) copy-start(s32[5]{0:T(128)} %offs.1) | copy-start | bytes 64

commit v2 on v1

v2 whole, which is shorter than its diff:
```python
import jax
import jax.numpy as jnp
from jax import lax
from jax.experimental import pallas as pl
from jax.experimental.pallas import tpu as pltpu
from jax.sharding import PartitionSpec as P

BLK = 128
REACH = 3
CHUNKS = 1


def weight_kernel(band, offs, table, out):
    nblk = band.shape[0]
    taps = offs.shape[0]
    for s in range(nblk):
        for k in range(taps):
            source = jnp.clip(s - offs[k], 0, nblk - 1)
            out[s, k * BLK : (k + 1) * BLK, :] = table[band[source], k]


def lat_kernel(chunk, coef, offs, lev, own, below, above, weights, out, blocks):
    variables, _, rows, nlat = own.shape
    nblk = nlat // BLK
    levels = coef.shape[1]
    taps = offs.shape[0]
    level = lev[0]
    lower = jnp.maximum(level - 1, 0)
    upper = jnp.minimum(level + 1, levels - 1)
    zeros = jnp.zeros(blocks.shape[1:], blocks.dtype)
    for edge in range(REACH):
        blocks[edge] = zeros
        blocks[REACH + nblk + edge] = zeros
    for n in range(variables):
        v = chunk * variables + n
        c_below = jnp.where(level > 0, coef[v, lower, 2], 0.0)
        c_own = coef[v, level, 1]
        c_above = jnp.where(level < levels - 1, coef[v, upper, 0], 0.0)
        for t in range(nblk):
            cols = slice(t * BLK, (t + 1) * BLK)
            total = c_below * below[n, 0, :, cols].astype(jnp.float32)
            total = total + c_own * own[n, 0, :, cols].astype(jnp.float32)
            total = total + c_above * above[n, 0, :, cols].astype(jnp.float32)
            blocks[REACH + t, n * rows : (n + 1) * rows, :] = total.astype(blocks.dtype)
    for s in range(nblk):
        lhs = [blocks[s - offs[k] + REACH] for k in range(taps)]
        total = jnp.dot(
            jnp.concatenate(lhs, axis=1), weights[s], preferred_element_type=jnp.float32
        )
        out[s * BLK : (s + 1) * BLK, :] = total.T.astype(out.dtype)


def lon_kernel(chunk, offs, data, weights, *refs):
    out, blocks, stage, sem = refs[-4:]
    peers, lats, width = data.shape
    half = BLK // 2
    variables = width // half
    nblk = peers // 2
    taps = offs.shape[0]
    group = 8
    first = lax.broadcasted_iota(jnp.int32, (lats, BLK), 1) < half
    for t in range(nblk):
        for pair in range(variables // 2):
            cols = slice(pair * BLK, (pair + 1) * BLK)
            a = data[2 * t, :, cols].astype(jnp.float32)
            b = data[2 * t + 1, :, cols].astype(jnp.float32)
            even = jnp.where(first, a, pltpu.roll(b, half, 1))
            odd = jnp.where(first, pltpu.roll(a, half, 1), b)
            v = 2 * pair
            blocks[t, v * lats : (v + 1) * lats, :] = even.astype(blocks.dtype)
            blocks[t, (v + 1) * lats : (v + 2) * lats, :] = odd.astype(blocks.dtype)
    rhs = jnp.concatenate([weights[k] for k in range(taps)], axis=0)
    rows = variables * lats
    for g in range(0, nblk, group):
        lhs = []
        for s in range(g, g + group):
            lhs.append(
                jnp.concatenate(
                    [blocks[lax.rem(s - offs[k] + nblk, nblk)] for k in range(taps)], axis=1
                )
            )
        total = jnp.dot(
            jnp.concatenate(lhs, axis=0), rhs, preferred_element_type=jnp.float32
        )
        for n, s in enumerate(range(g, g + group)):
            stage[s] = total[n * rows : (n + 1) * rows]
            for v in range(variables):
                pltpu.make_async_copy(
                    stage.at[s, v * lats : (v + 1) * lats],
                    out.at[:, chunk * variables + v, s, 0, :],
                    sem,
                ).start()
    pltpu.make_async_copy(stage, stage, sem).wait()


def per_device(
    increment, vert_coef, latitude_block_matrix, lat_band, lat_offsets, lon_blocks, lon_offsets
):
    variables, _, rows, nlat = increment.shape
    nblk = nlat // BLK
    npencil = lax.axis_size("pencil")
    nlev = lax.axis_size("lev")
    nlon = rows * npencil
    lats = nlat // npencil
    taps = lat_offsets.shape[0]
    each = variables // CHUNKS
    smem = pl.BlockSpec(memory_space=pltpu.SMEM)
    vmem = pl.BlockSpec(memory_space=pltpu.VMEM)
    hbm = pl.BlockSpec(memory_space=pl.ANY)
    up = [(n, n + 1) for n in range(nlev - 1)]
    down = [(n + 1, n) for n in range(nlev - 1)]
    own_level = lax.axis_index("lev").astype(jnp.int32).reshape(1)
    params = pltpu.CompilerParams(vmem_limit_bytes=32 * 2**20)

    parts = [increment[c * each : (c + 1) * each] for c in range(CHUNKS)]
    below = [lax.ppermute(part, "lev", up) for part in parts]
    above = [lax.ppermute(part, "lev", down) for part in parts]

    weights = pl.pallas_call(
        weight_kernel,
        out_shape=jax.ShapeDtypeStruct((nblk, taps * BLK, BLK), jnp.bfloat16),
        in_specs=[smem, smem, vmem],
        out_specs=vmem,
        compiler_params=params,
        name="latitude_weights",
    )(lat_band, lat_offsets, latitude_block_matrix)

    width = each * rows
    moved = []
    for c in range(CHUNKS):
        filtered = pl.pallas_call(
            lambda *refs, c=c: lat_kernel(c, *refs),
            out_shape=jax.ShapeDtypeStruct((nlat, width), jnp.bfloat16),
            in_specs=[smem] * 3 + [vmem] * 4,
            out_specs=vmem,
            scratch_shapes=[pltpu.VMEM((nblk + 2 * REACH, width, BLK), jnp.bfloat16)],
            compiler_params=params,
            cost_estimate=pl.CostEstimate(
                flops=2 * nlat * width * taps * BLK,
                bytes_accessed=8 * nlat * width,
                transcendentals=0,
            ),
            name=f"latitude_{c}",
        )(vert_coef, lat_offsets, own_level, parts[c], below[c], above[c], weights)
        moved.append(
            lax.all_to_all(filtered, "pencil", split_axis=0, concat_axis=0, tiled=True)
        )

    nout = nlon // BLK
    result = ()
    for c in range(CHUNKS):
        result = (
            pl.pallas_call(
                lambda *refs, c=c: lon_kernel(c, *refs),
                out_shape=jax.ShapeDtypeStruct((lats, variables, nout, 1, BLK), jnp.float32),
                in_specs=[smem, vmem, vmem] + [hbm] * len(result),
                out_specs=hbm,
                scratch_shapes=[
                    pltpu.VMEM((nout, lats * each, BLK), jnp.bfloat16),
                    pltpu.VMEM((nout, lats * each, BLK), jnp.float32),
                    pltpu.SemaphoreType.DMA,
                ],
                input_output_aliases={3: 0} if result else {},
                compiler_params=params,
                cost_estimate=pl.CostEstimate(
                    flops=2 * nlon * lats * each * taps * BLK,
                    bytes_accessed=6 * nlat * width,
                    transcendentals=0,
                ),
                name=f"longitude_{c}",
            )(lon_offsets, moved[c].reshape(npencil, lats, width), lon_blocks, *result),
        )
    return result[0].reshape(lats, variables, 1, nlon)


def solution(mesh):
    in_specs = (P(None, "lev", "pencil", None), P(), P(), P(), P(), P(), P())
    out_specs = P("pencil", None, "lev", None)
    return jax.shard_map(
        per_device, mesh=mesh, in_specs=in_specs, out_specs=out_specs, check_vma=False
    )
```

time: 65.7 us -> 59.6 us (0.907)
  waiting for transfers between devices: 15.1 us -> 11.7 us
  Pallas kernels: 8.23 us -> 6.73 us
  local copies, waits for them, and re-layouts: 4.66 us -> 3.44 us
    ppermute x2, waiting for transfers between devices: 15.1 us -> 11.7 us  [the longest x1 5.92 us: per_device(): below = [lax.ppermute(part, 'lev', up) for part in parts]]
    pallas_call x2 -> x3, Pallas kernels: 8.23 us -> 6.73 us  [the longest x1 3.12 us: per_device(): pl.pallas_call(lambda *refs, c=c: lon_kernel(c, *refs), out_shape=jax.Sha...]
    unnamed x13, local copies, waits for them, and re-layouts: 4.66 us -> 3.44 us
  transfers between devices with their start and end apart: 2 -> 2, of which waited for: 2 -> 2; matrix products, arithmetic and copies ran while one was open for 1% -> 1% of each run, Pallas kernels for 0% -> 1%
where the time goes in v2:
time: 59.6 us; the launch traced here: 59.3 us
  blocking collectives  29.2 us (49%)
  waiting for transfers between devices  11.7 us (20%)
  starting transfers between devices  8.13 us (14%)
  Pallas kernels  6.73 us (11%)
  local copies, waits for them, and re-layouts  3.44 us (6%)
    all_to_all x1, blocking collectives, per_device(): lax.all_to_all(filtered, 'pencil', split_axis=0, concat_axis=0, tiled=True)  29.2 us
    ppermute x1, starting transfers between devices, per_device(): below = [lax.ppermute(part, 'lev', up) for part in parts]  6.2 us
    ppermute x1, waiting for transfers between devices, per_device(): below = [lax.ppermute(part, 'lev', up) for part in parts]  5.92 us
    ppermute x1, waiting for transfers between devices, per_device(): above = [lax.ppermute(part, 'lev', down) for part in parts]  5.8 us
    unnamed x13, local copies, waits for them, and re-layouts  3.44 us
    pallas_call x1, Pallas kernels, per_device(): pl.pallas_call(lambda *refs, c=c: lon_kernel(c, *refs), out_shape=jax.Sha...  3.12 us
    pallas_call x1, Pallas kernels, per_device(): pl.pallas_call(lambda *refs, c=c: lat_kernel(c, *refs), out_shape=jax.Sha...  2.87 us
    ppermute x1, starting transfers between devices, per_device(): above = [lax.ppermute(part, 'lev', down) for part in parts]  1.92 us
  transfers between devices with their start and end apart: 2, of which 2 were waited for; matrix products, arithmetic and copies ran while one was open for 1% of the time, Pallas kernels for 1%

profile of v2, /device:TPU:1, one launch (start us, length us, event | category | flops | bytes accessed | tf_op | source)
XLA Modules:
  0.0 59.3 jit_solution(7852021027050825119)
XLA Ops:
  0.0 6.2 %collective-permute-start = (bf16[4,1,64,2048]{3,2,1,0:T(8,128)(2,1)}, bf16[4,1,64,2048]{3,2,1,0:T(8,128)(2,1)S(1)}, u32[]{:S(2)}, u32[]{:S(2)}) collective-permute-start(bf16[4,1,64,2048]{3,2,1,0:T(8,128)(2,1)} %refs_3_.1), channel_id=1, source_target_pairs={{0,1},{1,2},{2,3},{4,5},{5,6},{6,7},{8,9},{9,10},{10,11},{12,13},{... | collective-permute-start | bytes 3145736 | tf_op jit(solution)/shard_map/ppermute | solution.py:116
  6.2 1.9 %collective-permute-start.1 = (bf16[4,1,64,2048]{3,2,1,0:T(8,128)(2,1)}, bf16[4,1,64,2048]{3,2,1,0:T(8,128)(2,1)S(1)}, u32[]{:S(2)}, u32[]{:S(2)}) collective-permute-start(bf16[4,1,64,2048]{3,2,1,0:T(8,128)(2,1)} %refs_3_.1), channel_id=1, source_target_pairs={{1,0},{2,1},{3,2},{5,4},{6,5},{7,6},{9,8},{10,9},{11,10},{13,12},{... | collective-permute-start | bytes 3145736 | tf_op jit(solution)/shard_map/ppermute | solution.py:117
  8.1 0.8 %copy.8.refs_0_ = f32[4,4,3]{2,1,0:T(4,128)S(1)} copy(f32[4,4,3]{1,0,2:T(4,128)} %param.8) | data formatting | bytes 384 | tf_op args[1]
  8.9 0.0 copy-start
  8.9 1.3 %copy-done = bf16[8,5,128,128]{3,2,1,0:T(8,128)(2,1)S(1)} copy-done((bf16[8,5,128,128]{3,2,1,0:T(8,128)(2,1)S(1)}, bf16[8,5,128,128]{3,2,1,0:T(8,128)(2,1)}, u32[]{:S(2)}) %copy-start) | copy-done | bytes 1310744
  10.3 0.0 copy-start.3
  10.3 0.7 %copy-done.3 = s32[5]{0:T(128)S(1)} copy-done((s32[5]{0:T(128)S(1)}, s32[5]{0:T(128)}, u32[]{:S(2)}) %copy-start.3) | copy-done | bytes 44
  10.9 0.0 copy-start.4
  10.9 0.7 %copy-done.4 = s32[16]{0:T(128)S(1)} copy-done((s32[16]{0:T(128)S(1)}, s32[16]{0:T(128)}, u32[]{:S(2)}) %copy-start.4) | copy-done | bytes 88
  11.6 0.0 copy-start.1
  11.6 0.7 %latitude_weights.1.refs_6_ = bf16[16,640,128]{2,1,0:T(8,128)(2,1)S(1)} custom-call(s32[16]{0:T(128)S(1)} %copy-done.4, s32[5]{0:T(128)S(1)} %copy-done.3, bf16[8,5,128,128]{3,2,1,0:T(8,128)(2,1)S(1)} %copy-done), custom_call_target="tpu_custom_call" | custom-call | tf_op jit(solution)/shard_map/latitude_weights/pallas_call | solution.py:119
  12.3 5.9 %collective-permute-done.refs_4_ = bf16[4,1,64,2048]{3,2,1,0:T(8,128)(2,1)S(1)} collective-permute-done((bf16[4,1,64,2048]{3,2,1,0:T(8,128)(2,1)}, bf16[4,1,64,2048]{3,2,1,0:T(8,128)(2,1)S(1)}, u32[]{:S(2)}, u32[]{:S(2)}) %collective-permute-start) | collective-permute-done | bytes 1048608 | tf_op jit(solution)/shard_map/ppermute | solution.py:116
  18.2 5.8 %collective-permute-done.1.refs_5_ = bf16[4,1,64,2048]{3,2,1,0:T(8,128)(2,1)S(1)} collective-permute-done((bf16[4,1,64,2048]{3,2,1,0:T(8,128)(2,1)}, bf16[4,1,64,2048]{3,2,1,0:T(8,128)(2,1)S(1)}, u32[]{:S(2)}, u32[]{:S(2)}) %collective-permute-start.1) | collective-permute-done | bytes 1048608 | tf_op jit(solution)/shard_map/ppermute | solution.py:117
  24.0 0.0 copy-done.1
  24.0 2.9 %latitude_0.1 = bf16[2048,256]{1,0:T(8,128)(2,1)S(1)} custom-call(f32[4,4,3]{2,1,0:T(4,128)S(1)} %copy.8.refs_0_, s32[5]{0:T(128)S(1)} %copy-done.3, s32[1]{0:T(128)} %bitcast.refs_2_, bf16[4,1,64,2048]{3,2,1,0:T(8,128)(2,1)S(1)} %copy-done.1, bf16[4,1,64,2048]{3,2,1,0:T(8,128)(2,1)S(1)} %collective-permute-done.refs_4_, ...), custom_call_target="tpu_custom_call" | custom-call | flops 671088640 | bytes 4194304 | tf_op jit(solution)/shard_map/latitude_0/pallas_call | solution.py:131
  26.9 0.0 copy-start.2
  26.9 0.0 copy-start.5
  26.9 29.2 %all_to_all.9.refs_1_ = bf16[64,32,256]{2,1,0:T(8,128)(2,1)S(1)} all-to-all(bf16[64,32,256]{2,1,0:T(8,128)(2,1)S(1)} %bitcast.3), channel_id=1, replica_groups=mesh['pencil'=64,'lev'=4] {'pencil'}, dimensions={0} | all-to-all | bytes 2097152 | tf_op jit(solution)/shard_map/all_to_all | solution.py:146
  56.2 0.0 copy-done.2
  56.2 0.0 copy-done.5
  56.2 3.1 %longitude_0.1 = f32[32,4,32,1,128]{4,3,2,1,0:T(1,128)} custom-call(s32[5]{0:T(128)S(1)} %copy-done.5, bf16[64,32,256]{2,1,0:T(8,128)(2,1)S(1)} %all_to_all.9.refs_1_, bf16[5,128,128]{2,1,0:T(8,128)(2,1)S(1)} %copy-done.2), custom_call_target="tpu_custom_call" | custom-call | flops 671088640 | bytes 3145728 | tf_op jit(solution)/shard_map/longitude_0/pallas_call | solution.py:153
Async XLA Ops:
  0.0 18.2 %collective-permute-start = (bf16[4,1,64,2048]{3,2,1,0:T(8,128)(2,1)}, bf16[4,1,64,2048]{3,2,1,0:T(8,128)(2,1)S(1)}, u32[]{:S(2)}, u32[]{:S(2)}) collective-permute-start(bf16[4,1,64,2048]{3,2,1,0:T(8,128)(2,1)} %refs_3_.1), channel_id=1, source_target_pairs={{0,1},{1,2},{2,3},{4,5},{5,6},{6,7},{8,9},{9,10},{10,11},{12,13},{... | collective-permute-start | bytes 3145736 | tf_op jit(solution)/shard_map/ppermute | solution.py:116
  6.2 17.8 %collective-permute-start.1 = (bf16[4,1,64,2048]{3,2,1,0:T(8,128)(2,1)}, bf16[4,1,64,2048]{3,2,1,0:T(8,128)(2,1)S(1)}, u32[]{:S(2)}, u32[]{:S(2)}) collective-permute-start(bf16[4,1,64,2048]{3,2,1,0:T(8,128)(2,1)} %refs_3_.1), channel_id=1, source_target_pairs={{1,0},{2,1},{3,2},{5,4},{6,5},{7,6},{9,8},{10,9},{11,10},{13,12},{... | collective-permute-start | bytes 3145736 | tf_op jit(solution)/shard_map/ppermute | solution.py:117
  8.9 1.3 %copy-start = (bf16[8,5,128,128]{3,2,1,0:T(8,128)(2,1)S(1)}, bf16[8,5,128,128]{3,2,1,0:T(8,128)(2,1)}, u32[]{:S(2)}) copy-start(bf16[8,5,128,128]{3,2,1,0:T(8,128)(2,1)} %table.1) | copy-start | bytes 3932164
  10.3 0.7 %copy-start.3 = (s32[5]{0:T(128)S(1)}, s32[5]{0:T(128)}, u32[]{:S(2)}) copy-start(s32[5]{0:T(128)} %refs_1_.1) | copy-start | bytes 64
  10.9 0.7 %copy-start.4 = (s32[16]{0:T(128)S(1)}, s32[16]{0:T(128)}, u32[]{:S(2)}) copy-start(s32[16]{0:T(128)} %band.1) | copy-start | bytes 196
  11.6 12.5 %copy-start.1 = (bf16[4,1,64,2048]{3,2,1,0:T(8,128)(2,1)S(1)}, bf16[4,1,64,2048]{3,2,1,0:T(8,128)(2,1)}, u32[]{:S(2)}) copy-start(bf16[4,1,64,2048]{3,2,1,0:T(8,128)(2,1)} %refs_3_.1) | copy-start | bytes 3145732
  26.9 29.3 %copy-start.2 = (bf16[5,128,128]{2,1,0:T(8,128)(2,1)S(1)}, bf16[5,128,128]{2,1,0:T(8,128)(2,1)}, u32[]{:S(2)}) copy-start(bf16[5,128,128]{2,1,0:T(8,128)(2,1)} %refs_2_.1) | copy-start | bytes 491524
  26.9 29.3 %copy-start.5 = (s32[5]{0:T(128)S(1)}, s32[5]{0:T(128)}, u32[]{:S(2)}) copy-start(s32[5]{0:T(128)} %refs_0_.2) | copy-start | bytes 64

commit v3 on v1

v3 whole, which is shorter than its diff:
```python
import jax
import jax.numpy as jnp
from jax import lax
from jax.experimental import pallas as pl
from jax.experimental.pallas import tpu as pltpu
from jax.sharding import PartitionSpec as P

BLK = 128
REACH = 3
SPAN = 2 * REACH + 2


def operator_kernel(
    band_hbm, lat_offs_hbm, lon_offs_hbm, coef_hbm, table_hbm, lon_hbm,
    lat_out, lon_out, coef_out,
    band, lat_offs, lon_offs, coef, table, lon, sems,
):
    moves = [
        pltpu.make_async_copy(source, target, sems.at[n])
        for n, (source, target) in enumerate(
            (
                (band_hbm, band),
                (lat_offs_hbm, lat_offs),
                (lon_offs_hbm, lon_offs),
                (coef_hbm, coef),
                (table_hbm, table),
                (lon_hbm, lon),
            )
        )
    ]
    for move in moves:
        move.start()
    level = lax.axis_index("lev")
    lat_out[...] = jnp.zeros_like(lat_out)
    lon_out[...] = jnp.zeros_like(lon_out)
    for move in moves:
        move.wait()
    variables, levels, _ = coef.shape
    taps = lat_offs.shape[0]
    nblk = band.shape[0]
    lower = jnp.maximum(level - 1, 0)
    upper = jnp.minimum(level + 1, levels - 1)
    even = lax.rem(level, 2) == 0
    for v in range(variables):
        below = jnp.where(level > 0, coef[v, lower, 2], 0.0)
        above = jnp.where(level < levels - 1, coef[v, upper, 0], 0.0)
        mine = (coef[v, level, 1], jnp.where(even, above, below), jnp.where(even, below, above))
        for n in range(3):
            coef_out[3 * v + n : 3 * v + n + 1, :] = jnp.full((1, BLK), mine[n], jnp.float32)
    for k in range(taps):
        place = REACH - lon_offs[k]
        for half in range(2):
            rows = pl.ds(pl.multiple_of((place + half) * BLK, BLK), BLK)
            lon_out[rows, half * BLK : (half + 1) * BLK] = lon[k]
    for s in range(nblk):
        half = s % 2
        for k in range(taps):
            source = jnp.clip(s - lat_offs[k], 0, nblk - 1)
            place = REACH - lat_offs[k] + half
            rows = pl.ds(pl.multiple_of(place * BLK, BLK), BLK)
            lat_out[s // 2, rows, half * BLK : (half + 1) * BLK] = table[band[source], k]


def lat_kernel(own, chip, cross, coef, weights, out, rows_of):
    variables, _, rows, nlat = own.shape
    nblk = nlat // BLK
    zeros = jnp.zeros((variables * rows, REACH * BLK), rows_of.dtype)
    rows_of[:, : REACH * BLK] = zeros
    rows_of[:, (REACH + nblk) * BLK :] = zeros
    done = 0
    for pair in range(nblk // 2):
        ready = min(nblk, 2 * pair + SPAN - REACH)
        for t in range(done, ready):
            cols = slice(t * BLK, (t + 1) * BLK)
            for v in range(variables):
                total = coef[3 * v : 3 * v + 1, :] * own[v, 0, :, cols].astype(jnp.float32)
                total = total + coef[3 * v + 1 : 3 * v + 2, :] * chip[v, 0, :, cols].astype(
                    jnp.float32
                )
                total = total + coef[3 * v + 2 : 3 * v + 3, :] * cross[v, 0, :, cols].astype(
                    jnp.float32
                )
                rows_of[
                    v * rows : (v + 1) * rows, (REACH + t) * BLK : (REACH + t + 1) * BLK
                ] = total.astype(rows_of.dtype)
        done = ready
        total = jnp.dot(
            rows_of[:, 2 * pair * BLK : (2 * pair + SPAN) * BLK],
            weights[pair],
            preferred_element_type=jnp.float32,
        )
        out[2 * pair * BLK : 2 * (pair + 1) * BLK, :] = total.T.astype(out.dtype)


def lon_kernel(data, weights, out, rows_of, stage, sem):
    peers, lats, width = data.shape
    half = BLK // 2
    variables = width // half
    nblk = peers // 2
    rows = variables * lats
    first = lax.broadcasted_iota(jnp.int32, (lats, BLK), 1) < half
    group = 4

    def fill(t):
        spots = [p for p in (t + REACH, t + REACH + nblk, t + REACH - nblk) if 0 <= p]
        spots = [p for p in spots if p < nblk + 2 * REACH]
        for pair in range(variables // 2):
            cols = slice(pair * BLK, (pair + 1) * BLK)
            a = data[2 * t, :, cols].astype(jnp.float32)
            b = data[2 * t + 1, :, cols].astype(jnp.float32)
            even = jnp.where(first, a, pltpu.roll(b, half, 1)).astype(rows_of.dtype)
            odd = jnp.where(first, pltpu.roll(a, half, 1), b).astype(rows_of.dtype)
            v = 2 * pair
            for p in spots:
                rows_of[v * lats : (v + 1) * lats, p * BLK : (p + 1) * BLK] = even
                rows_of[(v + 1) * lats : (v + 2) * lats, p * BLK : (p + 1) * BLK] = odd

    order = [*range(nblk - REACH, nblk), *range(nblk - REACH)]
    done = 0
    for g in range(0, nblk // 2, group):
        ready = min(nblk, 2 * (g + group) + 2 * REACH)
        for t in order[done:ready]:
            fill(t)
        done = ready
        lhs = jnp.concatenate(
            [
                rows_of[:, 2 * pair * BLK : (2 * pair + SPAN) * BLK]
                for pair in range(g, g + group)
            ],
            axis=0,
        )
        total = jnp.dot(lhs, weights[...], preferred_element_type=jnp.float32)
        for n in range(group):
            for h in range(2):
                s = 2 * (g + n) + h
                stage[s] = total[n * rows : (n + 1) * rows, h * BLK : (h + 1) * BLK]
                for v in range(variables):
                    pltpu.make_async_copy(
                        stage.at[s, v * lats : (v + 1) * lats], out.at[:, v, s, 0, :], sem
                    ).start()
    pltpu.make_async_copy(stage, stage, sem).wait()


def per_device(
    increment, vert_coef, latitude_block_matrix, lat_band, lat_offsets, lon_blocks, lon_offsets
):
    variables, _, rows, nlat = increment.shape
    nblk = nlat // BLK
    npencil = lax.axis_size("pencil")
    nlev = lax.axis_size("lev")
    nlon = rows * npencil
    lats = nlat // npencil
    width = variables * rows
    nout = nlon // BLK
    vmem = pl.BlockSpec(memory_space=pltpu.VMEM)
    hbm = pl.BlockSpec(memory_space=pl.ANY)
    params = pltpu.CompilerParams(vmem_limit_bytes=32 * 2**20)

    chip_pairs = [(n, n ^ 1) for n in range(nlev)]
    cross_pairs = [p for n in range(1, nlev - 1, 2) for p in ((n, n + 1), (n + 1, n))]
    chip = lax.ppermute(increment, "lev", chip_pairs)
    cross = lax.ppermute(increment, "lev", cross_pairs)

    lat_weights, lon_weights, coef = pl.pallas_call(
        operator_kernel,
        out_shape=(
            jax.ShapeDtypeStruct((nblk // 2, SPAN * BLK, 2 * BLK), jnp.bfloat16),
            jax.ShapeDtypeStruct((SPAN * BLK, 2 * BLK), jnp.bfloat16),
            jax.ShapeDtypeStruct((16, BLK), jnp.float32),
        ),
        in_specs=[pl.BlockSpec(memory_space=pltpu.HBM)] * 6,
        out_specs=(vmem,) * 3,
        scratch_shapes=[
            pltpu.SMEM(lat_band.shape, jnp.int32),
            pltpu.SMEM(lat_offsets.shape, jnp.int32),
            pltpu.SMEM(lon_offsets.shape, jnp.int32),
            pltpu.SMEM(vert_coef.shape, jnp.float32),
            pltpu.VMEM(latitude_block_matrix.shape, jnp.bfloat16),
            pltpu.VMEM(lon_blocks.shape, jnp.bfloat16),
            pltpu.SemaphoreType.DMA((6,)),
        ],
        compiler_params=params,
        name="operators",
    )(lat_band, lat_offsets, lon_offsets, vert_coef, latitude_block_matrix, lon_blocks)

    filtered = pl.pallas_call(
        lat_kernel,
        out_shape=jax.ShapeDtypeStruct((nlat, width), jnp.bfloat16),
        in_specs=[vmem] * 5,
        out_specs=vmem,
        scratch_shapes=[pltpu.VMEM((width, nlat + 2 * REACH * BLK), jnp.bfloat16)],
        compiler_params=params,
        name="latitude",
    )(increment, chip, cross, coef, lat_weights)
    moved = lax.all_to_all(filtered, "pencil", split_axis=0, concat_axis=0, tiled=True)
    result = pl.pallas_call(
        lon_kernel,
        out_shape=jax.ShapeDtypeStruct((lats, variables, nout, 1, BLK), jnp.float32),
        in_specs=[vmem] * 2,
        out_specs=hbm,
        scratch_shapes=[
            pltpu.VMEM((lats * variables, (nout + 2 * REACH) * BLK), jnp.bfloat16),
            pltpu.VMEM((nout, lats * variables, BLK), jnp.float32),
            pltpu.SemaphoreType.DMA,
        ],
        compiler_params=params,
        name="longitude",
    )(moved.reshape(npencil, lats, width), lon_weights)
    return result.reshape(lats, variables, 1, nlon)


def solution(mesh):
    in_specs = (P(None, "lev", "pencil", None), P(), P(), P(), P(), P(), P())
    out_specs = P("pencil", None, "lev", None)
    return jax.shard_map(
        per_device, mesh=mesh, in_specs=in_specs, out_specs=out_specs, check_vma=False
    )
```

time: 65.7 us -> 54.7 us (0.83)
  waiting for transfers between devices: 15.1 us -> 8.4 us
  Pallas kernels: 8.23 us -> 5.25 us
  starting transfers between devices: 8.13 us -> 6.21 us
    ppermute x2, waiting for transfers between devices: 15.1 us -> 8.4 us  [the longest x1 8.4 us: per_device(): cross = lax.ppermute(increment, 'lev', cross_pairs)]
    pallas_call x2 -> x3, Pallas kernels: 8.23 us -> 5.25 us  [the longest x1 2.25 us: per_device(): pl.pallas_call(lon_kernel, out_shape=jax.ShapeDtypeStruct((lats, variable...]
    ppermute x2, starting transfers between devices: 8.13 us -> 6.21 us  [the longest x1 3.24 us: per_device(): chip = lax.ppermute(increment, 'lev', chip_pairs)]
  transfers between devices with their start and end apart: 2 -> 2, of which waited for: 2 -> 1; matrix products, arithmetic and copies ran while one was open for 1% -> 1% of each run, Pallas kernels for 0% -> 3%
where the time goes in v3:
time: 54.7 us; the launch traced here: 54.5 us
  blocking collectives  29.6 us (54%)
  waiting for transfers between devices  8.4 us (15%)
  starting transfers between devices  6.21 us (11%)
  Pallas kernels  5.25 us (10%)
  local copies, waits for them, and re-layouts  5 us (9%)
    all_to_all x1, blocking collectives, per_device(): lax.all_to_all(filtered, 'pencil', split_axis=0, concat_axis=0, tiled=True)  29.6 us
    ppermute x1, waiting for transfers between devices, per_device(): cross = lax.ppermute(increment, 'lev', cross_pairs)  8.4 us
    unnamed x13, local copies, waits for them, and re-layouts  5 us
    ppermute x1, starting transfers between devices, per_device(): chip = lax.ppermute(increment, 'lev', chip_pairs)  3.24 us
    ppermute x1, starting transfers between devices, per_device(): cross = lax.ppermute(increment, 'lev', cross_pairs)  2.97 us
    pallas_call x1, Pallas kernels, per_device(): pl.pallas_call(lon_kernel, out_shape=jax.ShapeDtypeStruct((lats, variable...  2.25 us
    pallas_call x1, Pallas kernels, per_device(): pl.pallas_call(lat_kernel, out_shape=jax.ShapeDtypeStruct((nlat, width),...  1.57 us
    pallas_call x1, Pallas kernels, per_device(): pl.pallas_call(operator_kernel, out_shape=(jax.ShapeDtypeStruct((nblk //...  1.44 us
  transfers between devices with their start and end apart: 2, of which 1 were waited for; matrix products, arithmetic and copies ran while one was open for 1% of the time, Pallas kernels for 3%

profile of v3, /device:TPU:1, one launch (start us, length us, event | category | flops | bytes accessed | tf_op | source)
XLA Modules:
  0.0 54.5 jit_solution(12566589759601046879)
XLA Ops:
  0.0 3.2 %collective-permute-start = (bf16[4,1,64,2048]{3,2,1,0:T(8,128)(2,1)}, bf16[4,1,64,2048]{3,2,1,0:T(8,128)(2,1)S(1)}, u32[]{:S(2)}, u32[]{:S(2)}) collective-permute-start(bf16[4,1,64,2048]{3,2,1,0:T(8,128)(2,1)} %own.1), channel_id=1, source_target_pairs={{0,1},{1,0},{2,3},{3,2},{4,5},{5,4},{6,7},{7,6},{8,9},{9,8},{10,11... | collective-permute-start | bytes 3145736 | tf_op jit(solution)/shard_map/ppermute | solution.py:161
  3.2 3.0 %collective-permute-start.1 = (bf16[4,1,64,2048]{3,2,1,0:T(8,128)(2,1)}, bf16[4,1,64,2048]{3,2,1,0:T(8,128)(2,1)S(1)}, u32[]{:S(2)}, u32[]{:S(2)}) collective-permute-start(bf16[4,1,64,2048]{3,2,1,0:T(8,128)(2,1)} %own.1), channel_id=1, source_target_pairs={{1,2},{2,1},{5,6},{6,5},{9,10},{10,9},{13,14},{14,13},{17,18},{18,... | collective-permute-start | bytes 3145736 | tf_op jit(solution)/shard_map/ppermute | solution.py:162
  6.2 0.8 %copy.8.coef_hbm = f32[4,4,3]{2,1,0:T(4,128)S(1)} copy(f32[4,4,3]{1,0,2:T(4,128)} %param.8) | data formatting | bytes 384 | tf_op args[1]
  7.0 0.0 copy-start
  7.0 1.3 %copy-done = bf16[8,5,128,128]{3,2,1,0:T(8,128)(2,1)S(1)} copy-done((bf16[8,5,128,128]{3,2,1,0:T(8,128)(2,1)S(1)}, bf16[8,5,128,128]{3,2,1,0:T(8,128)(2,1)}, u32[]{:S(2)}) %copy-start) | copy-done | bytes 1310744
  8.3 0.0 copy-start.2
  8.3 0.9 %copy-done.2 = bf16[5,128,128]{2,1,0:T(8,128)(2,1)S(1)} copy-done((bf16[5,128,128]{2,1,0:T(8,128)(2,1)S(1)}, bf16[5,128,128]{2,1,0:T(8,128)(2,1)}, u32[]{:S(2)}) %copy-start.2) | copy-done | bytes 163864
  9.2 0.0 copy-start.3
  9.2 0.7 %copy-done.3 = s32[16]{0:T(128)S(1)} copy-done((s32[16]{0:T(128)S(1)}, s32[16]{0:T(128)}, u32[]{:S(2)}) %copy-start.3) | copy-done | bytes 88
  9.9 0.0 copy-start.4
  9.9 0.7 %copy-done.4 = s32[5]{0:T(128)S(1)} copy-done((s32[5]{0:T(128)S(1)}, s32[5]{0:T(128)}, u32[]{:S(2)}) %copy-start.4) | copy-done | bytes 44
  10.6 0.0 copy-start.5
  10.6 0.7 %copy-done.5 = s32[5]{0:T(128)S(1)} copy-done((s32[5]{0:T(128)S(1)}, s32[5]{0:T(128)}, u32[]{:S(2)}) %copy-start.5) | copy-done | bytes 44
  11.2 0.0 copy-start.1
  11.2 1.4 %operators.1 = (bf16[8,1024,256]{2,1,0:T(8,128)(2,1)S(1)}, bf16[1024,256]{1,0:T(8,128)(2,1)S(1)}, f32[16,128]{1,0:T(8,128)S(1)}) custom-call(s32[16]{0:T(128)S(1)} %copy-done.3, s32[5]{0:T(128)S(1)} %copy-done.4, s32[5]{0:T(128)S(1)} %copy-done.5, f32[4,4,3]{2,1,0:T(4,128)S(1)} %copy.8.coef_hbm, bf16[8,5,128,128]{3,2,1,0:T(8,128)(2,1)S(1)} %copy-done, ...), custom_call_target="tpu_custom_call" | custom-call | tf_op jit(solution)/shard_map/operators/pallas_call | solution.py:164
  12.7 0.0 collective-permute-done.chip
  12.7 8.4 %collective-permute-done.1.cross = bf16[4,1,64,2048]{3,2,1,0:T(8,128)(2,1)S(1)} collective-permute-done((bf16[4,1,64,2048]{3,2,1,0:T(8,128)(2,1)}, bf16[4,1,64,2048]{3,2,1,0:T(8,128)(2,1)S(1)}, u32[]{:S(2)}, u32[]{:S(2)}) %collective-permute-start.1) | collective-permute-done | bytes 1048608 | tf_op jit(solution)/shard_map/ppermute | solution.py:162
  21.1 0.0 copy-done.1
  21.1 1.6 %latitude.1 = bf16[2048,256]{1,0:T(8,128)(2,1)S(1)} custom-call(bf16[4,1,64,2048]{3,2,1,0:T(8,128)(2,1)S(1)} %copy-done.1, bf16[4,1,64,2048]{3,2,1,0:T(8,128)(2,1)S(1)} %collective-permute-done.chip, bf16[4,1,64,2048]{3,2,1,0:T(8,128)(2,1)S(1)} %collective-permute-done.1.cross, f32[16,128]{1,0:T(8,128)S(1)} %get-tuple-element.8.coef, ...), custom_call_target="tpu_custom_call" | custom-call | tf_op jit(solution)/shard_map/latitude/pallas_call | solution.py:186
  22.6 29.6 %all_to_all.9.data = bf16[64,32,256]{2,1,0:T(8,128)(2,1)S(1)} all-to-all(bf16[64,32,256]{2,1,0:T(8,128)(2,1)S(1)} %bitcast.2), channel_id=1, replica_groups=mesh['pencil'=64,'lev'=4] {'pencil'}, dimensions={0} | all-to-all | bytes 2097152 | tf_op jit(solution)/shard_map/all_to_all | solution.py:195
  52.2 2.2 %longitude.1 = f32[32,4,32,1,128]{4,3,2,1,0:T(1,128)} custom-call(bf16[64,32,256]{2,1,0:T(8,128)(2,1)S(1)} %all_to_all.9.data, bf16[1024,256]{1,0:T(8,128)(2,1)S(1)} %get-tuple-element.10.weights), custom_call_target="tpu_custom_call" | custom-call | tf_op jit(solution)/shard_map/longitude/pallas_call | solution.py:196
Async XLA Ops:
  0.0 12.7 %collective-permute-start = (bf16[4,1,64,2048]{3,2,1,0:T(8,128)(2,1)}, bf16[4,1,64,2048]{3,2,1,0:T(8,128)(2,1)S(1)}, u32[]{:S(2)}, u32[]{:S(2)}) collective-permute-start(bf16[4,1,64,2048]{3,2,1,0:T(8,128)(2,1)} %own.1), channel_id=1, source_target_pairs={{0,1},{1,0},{2,3},{3,2},{4,5},{5,4},{6,7},{7,6},{8,9},{9,8},{10,11... | collective-permute-start | bytes 3145736 | tf_op jit(solution)/shard_map/ppermute | solution.py:161
  3.2 17.8 %collective-permute-start.1 = (bf16[4,1,64,2048]{3,2,1,0:T(8,128)(2,1)}, bf16[4,1,64,2048]{3,2,1,0:T(8,128)(2,1)S(1)}, u32[]{:S(2)}, u32[]{:S(2)}) collective-permute-start(bf16[4,1,64,2048]{3,2,1,0:T(8,128)(2,1)} %own.1), channel_id=1, source_target_pairs={{1,2},{2,1},{5,6},{6,5},{9,10},{10,9},{13,14},{14,13},{17,18},{18,... | collective-permute-start | bytes 3145736 | tf_op jit(solution)/shard_map/ppermute | solution.py:162
  7.0 1.3 %copy-start = (bf16[8,5,128,128]{3,2,1,0:T(8,128)(2,1)S(1)}, bf16[8,5,128,128]{3,2,1,0:T(8,128)(2,1)}, u32[]{:S(2)}) copy-start(bf16[8,5,128,128]{3,2,1,0:T(8,128)(2,1)} %table_hbm.1) | copy-start | bytes 3932164
  8.3 0.9 %copy-start.2 = (bf16[5,128,128]{2,1,0:T(8,128)(2,1)S(1)}, bf16[5,128,128]{2,1,0:T(8,128)(2,1)}, u32[]{:S(2)}) copy-start(bf16[5,128,128]{2,1,0:T(8,128)(2,1)} %lon_hbm.1) | copy-start | bytes 491524
  9.2 0.7 %copy-start.3 = (s32[16]{0:T(128)S(1)}, s32[16]{0:T(128)}, u32[]{:S(2)}) copy-start(s32[16]{0:T(128)} %band_hbm.1) | copy-start | bytes 196
  9.9 0.7 %copy-start.4 = (s32[5]{0:T(128)S(1)}, s32[5]{0:T(128)}, u32[]{:S(2)}) copy-start(s32[5]{0:T(128)} %lat_offs_hbm.1) | copy-start | bytes 64
  10.6 0.7 %copy-start.5 = (s32[5]{0:T(128)S(1)}, s32[5]{0:T(128)}, u32[]{:S(2)}) copy-start(s32[5]{0:T(128)} %lon_offs_hbm.1) | copy-start | bytes 64
  11.2 9.9 %copy-start.1 = (bf16[4,1,64,2048]{3,2,1,0:T(8,128)(2,1)S(1)}, bf16[4,1,64,2048]{3,2,1,0:T(8,128)(2,1)}, u32[]{:S(2)}) copy-start(bf16[4,1,64,2048]{3,2,1,0:T(8,128)(2,1)} %own.1) | copy-start | bytes 3145732

commit v4 on v3

--- a/solution.py
+++ b/solution.py
@@ -181,7 +181,19 @@
         ],
         compiler_params=params,
         name="operators",
-    )(lat_band, lat_offsets, lon_offsets, vert_coef, latitude_block_matrix, lon_blocks)
+    )(
+        *(
+            pltpu.with_memory_space_constraint(x, pltpu.HBM)
+            for x in (
+                lat_band,
+                lat_offsets,
+                lon_offsets,
+                vert_coef,
+                latitude_block_matrix,
+                lon_blocks,
+            )
+        )
+    )
 
     filtered = pl.pallas_call(
         lat_kernel,

time: 54.7 us -> 53.5 us (0.978)
  local copies, waits for them, and re-layouts: 5 us -> 1.39 us
  waiting for transfers between devices: 8.4 us -> 11.2 us
  blocking collectives: 29.6 us -> 28.5 us
    unnamed x13 -> x3, local copies, waits for them, and re-layouts: 5 us -> 1.39 us
    ppermute x1, waiting for transfers between devices: 8.4 us -> 11.2 us  [per_device(): cross = lax.ppermute(increment, 'lev', cross_pairs)]
    all_to_all x1, blocking collectives: 29.6 us -> 28.5 us  [per_device(): lax.all_to_all(filtered, 'pencil', split_axis=0, concat_axis=0, tiled=True)]
    pallas_call x1, Pallas kernels: 1.44 us -> 2.06 us  [per_device(): pl.pallas_call(operator_kernel, out_shape=(jax.ShapeDtypeStruct((nblk //...]
  transfers between devices with their start and end apart: 2 -> 2, of which waited for: 1 -> 1; matrix products, arithmetic and copies ran while one was open for 1% -> 3% of each run, Pallas kernels for 3% -> 4%
where the time goes in v4:
time: 53.5 us; the launch traced here: 53.3 us
  blocking collectives  28.5 us (53%)
  waiting for transfers between devices  11.2 us (21%)
  starting transfers between devices  6.34 us (12%)
  Pallas kernels  5.76 us (11%)
  local copies, waits for them, and re-layouts  1.39 us (3%)
    all_to_all x1, blocking collectives, per_device(): lax.all_to_all(filtered, 'pencil', split_axis=0, concat_axis=0, tiled=True)  28.5 us
    ppermute x1, waiting for transfers between devices, per_device(): cross = lax.ppermute(increment, 'lev', cross_pairs)  11.2 us
    ppermute x1, starting transfers between devices, per_device(): chip = lax.ppermute(increment, 'lev', chip_pairs)  3.24 us
    ppermute x1, starting transfers between devices, per_device(): cross = lax.ppermute(increment, 'lev', cross_pairs)  3.1 us
    pallas_call x1, Pallas kernels, per_device(): pl.pallas_call(lon_kernel, out_shape=jax.ShapeDtypeStruct((lats, variable...  2.25 us
    pallas_call x1, Pallas kernels, per_device(): pl.pallas_call(operator_kernel, out_shape=(jax.ShapeDtypeStruct((nblk //...  2.06 us
    pallas_call x1, Pallas kernels, per_device(): pl.pallas_call(lat_kernel, out_shape=jax.ShapeDtypeStruct((nlat, width),...  1.45 us
    unnamed x3, local copies, waits for them, and re-layouts  1.39 us
  transfers between devices with their start and end apart: 2, of which 1 were waited for; matrix products, arithmetic and copies ran while one was open for 3% of the time, Pallas kernels for 4%

profile of v4, /device:TPU:1, one launch (start us, length us, event | category | flops | bytes accessed | tf_op | source)
XLA Modules:
  0.0 53.3 jit_solution(12013492117509115798)
XLA Ops:
  0.0 0.0 copy-start
  0.0 3.2 %collective-permute-start = (bf16[4,1,64,2048]{3,2,1,0:T(8,128)(2,1)}, bf16[4,1,64,2048]{3,2,1,0:T(8,128)(2,1)S(1)}, u32[]{:S(2)}, u32[]{:S(2)}) collective-permute-start(bf16[4,1,64,2048]{3,2,1,0:T(8,128)(2,1)} %own.1), channel_id=1, source_target_pairs={{0,1},{1,0},{2,3},{3,2},{4,5},{5,4},{6,7},{7,6},{8,9},{9,8},{10,11... | collective-permute-start | bytes 3145736 | tf_op jit(solution)/shard_map/ppermute | solution.py:161
  3.2 3.1 %collective-permute-start.1 = (bf16[4,1,64,2048]{3,2,1,0:T(8,128)(2,1)}, bf16[4,1,64,2048]{3,2,1,0:T(8,128)(2,1)S(1)}, u32[]{:S(2)}, u32[]{:S(2)}) collective-permute-start(bf16[4,1,64,2048]{3,2,1,0:T(8,128)(2,1)} %own.1), channel_id=1, source_target_pairs={{1,2},{2,1},{5,6},{6,5},{9,10},{10,9},{13,14},{14,13},{17,18},{18,... | collective-permute-start | bytes 3145736 | tf_op jit(solution)/shard_map/ppermute | solution.py:162
  6.4 1.4 %copy.8.coef_hbm = f32[4,4,3]{2,1,0:T(4,128)} copy(f32[4,4,3]{1,0,2:T(4,128)} %param.8) | data formatting | bytes 384 | tf_op args[1]
  7.7 2.1 %operators.1 = (bf16[8,1024,256]{2,1,0:T(8,128)(2,1)S(1)}, bf16[1024,256]{1,0:T(8,128)(2,1)S(1)}, f32[16,128]{1,0:T(8,128)S(1)}) custom-call(s32[16]{0:T(128)} %band_hbm.1, s32[5]{0:T(128)} %lat_offs_hbm.1, s32[5]{0:T(128)} %lon_offs_hbm.1, f32[4,4,3]{2,1,0:T(4,128)} %copy.8.coef_hbm, bf16[8,5,128,128]{3,2,1,0:T(8,128)(2,1)} %table_hbm.1, ...), custom_call_target="tpu_custom_call" | custom-call | tf_op jit(solution)/shard_map/operators/pallas_call | solution.py:164
  9.8 0.0 collective-permute-done.chip
  9.8 11.2 %collective-permute-done.1.cross = bf16[4,1,64,2048]{3,2,1,0:T(8,128)(2,1)S(1)} collective-permute-done((bf16[4,1,64,2048]{3,2,1,0:T(8,128)(2,1)}, bf16[4,1,64,2048]{3,2,1,0:T(8,128)(2,1)S(1)}, u32[]{:S(2)}, u32[]{:S(2)}) %collective-permute-start.1) | collective-permute-done | bytes 1048608 | tf_op jit(solution)/shard_map/ppermute | solution.py:162
  21.1 0.0 copy-done
  21.1 1.5 %latitude.1 = bf16[2048,256]{1,0:T(8,128)(2,1)S(1)} custom-call(bf16[4,1,64,2048]{3,2,1,0:T(8,128)(2,1)S(1)} %copy-done, bf16[4,1,64,2048]{3,2,1,0:T(8,128)(2,1)S(1)} %collective-permute-done.chip, bf16[4,1,64,2048]{3,2,1,0:T(8,128)(2,1)S(1)} %collective-permute-done.1.cross, f32[16,128]{1,0:T(8,128)S(1)} %get-tuple-element.8.coef, ...), custom_call_target="tpu_custom_call" | custom-call | tf_op jit(solution)/shard_map/latitude/pallas_call | solution.py:198
  22.5 28.5 %all_to_all.9.data = bf16[64,32,256]{2,1,0:T(8,128)(2,1)S(1)} all-to-all(bf16[64,32,256]{2,1,0:T(8,128)(2,1)S(1)} %bitcast.2), channel_id=1, replica_groups=mesh['pencil'=64,'lev'=4] {'pencil'}, dimensions={0} | all-to-all | bytes 2097152 | tf_op jit(solution)/shard_map/all_to_all | solution.py:207
  51.0 2.3 %longitude.1 = f32[32,4,32,1,128]{4,3,2,1,0:T(1,128)} custom-call(bf16[64,32,256]{2,1,0:T(8,128)(2,1)S(1)} %all_to_all.9.data, bf16[1024,256]{1,0:T(8,128)(2,1)S(1)} %get-tuple-element.10.weights), custom_call_target="tpu_custom_call" | custom-call | tf_op jit(solution)/shard_map/longitude/pallas_call | solution.py:208
Async XLA Ops:
  0.0 21.1 %copy-start = (bf16[4,1,64,2048]{3,2,1,0:T(8,128)(2,1)S(1)}, bf16[4,1,64,2048]{3,2,1,0:T(8,128)(2,1)}, u32[]{:S(2)}) copy-start(bf16[4,1,64,2048]{3,2,1,0:T(8,128)(2,1)} %own.1) | copy-start | bytes 3145732
  0.0 9.8 %collective-permute-start = (bf16[4,1,64,2048]{3,2,1,0:T(8,128)(2,1)}, bf16[4,1,64,2048]{3,2,1,0:T(8,128)(2,1)S(1)}, u32[]{:S(2)}, u32[]{:S(2)}) collective-permute-start(bf16[4,1,64,2048]{3,2,1,0:T(8,128)(2,1)} %own.1), channel_id=1, source_target_pairs={{0,1},{1,0},{2,3},{3,2},{4,5},{5,4},{6,7},{7,6},{8,9},{9,8},{10,11... | collective-permute-start | bytes 3145736 | tf_op jit(solution)/shard_map/ppermute | solution.py:161
  3.2 17.8 %collective-permute-start.1 = (bf16[4,1,64,2048]{3,2,1,0:T(8,128)(2,1)}, bf16[4,1,64,2048]{3,2,1,0:T(8,128)(2,1)S(1)}, u32[]{:S(2)}, u32[]{:S(2)}) collective-permute-start(bf16[4,1,64,2048]{3,2,1,0:T(8,128)(2,1)} %own.1), channel_id=1, source_target_pairs={{1,2},{2,1},{5,6},{6,5},{9,10},{10,9},{13,14},{14,13},{17,18},{18,... | collective-permute-start | bytes 3145736 | tf_op jit(solution)/shard_map/ppermute | solution.py:162

commit v5 on v4

--- a/solution.py
+++ b/solution.py
@@ -99,7 +99,6 @@
     nblk = peers // 2
     rows = variables * lats
     first = lax.broadcasted_iota(jnp.int32, (lats, BLK), 1) < half
-    group = 4
 
     def fill(t):
         spots = [p for p in (t + REACH, t + REACH + nblk, t + REACH - nblk) if 0 <= p]
@@ -116,8 +115,8 @@
                 rows_of[(v + 1) * lats : (v + 2) * lats, p * BLK : (p + 1) * BLK] = odd
 
     order = [*range(nblk - REACH, nblk), *range(nblk - REACH)]
-    done = 0
-    for g in range(0, nblk // 2, group):
+    done = g = 0
+    for group in (1, 2, 3, 3, 3, 4):
         ready = min(nblk, 2 * (g + group) + 2 * REACH)
         for t in order[done:ready]:
             fill(t)
@@ -138,6 +137,8 @@
                     pltpu.make_async_copy(
                         stage.at[s, v * lats : (v + 1) * lats], out.at[:, v, s, 0, :], sem
                     ).start()
+        g += group
+    assert 2 * g == nblk
     pltpu.make_async_copy(stage, stage, sem).wait()
 
 

time: 53.5 us -> 53.3 us (level)
  no operation moved by 1% of the time
where the time goes in v5:
time: 53.3 us; the launch traced here: 53.1 us
  blocking collectives  28.5 us (53%)
  waiting for transfers between devices  11.2 us (21%)
  starting transfers between devices  6.34 us (12%)
  Pallas kernels  5.56 us (10%)
  local copies, waits for them, and re-layouts  1.39 us (3%)
    all_to_all x1, blocking collectives, per_device(): lax.all_to_all(filtered, 'pencil', split_axis=0, concat_axis=0, tiled=True)  28.5 us
    ppermute x1, waiting for transfers between devices, per_device(): cross = lax.ppermute(increment, 'lev', cross_pairs)  11.2 us
    ppermute x1, starting transfers between devices, per_device(): chip = lax.ppermute(increment, 'lev', chip_pairs)  3.24 us
    ppermute x1, starting transfers between devices, per_device(): cross = lax.ppermute(increment, 'lev', cross_pairs)  3.1 us
    pallas_call x1, Pallas kernels, per_device(): pl.pallas_call(operator_kernel, out_shape=(jax.ShapeDtypeStruct((nblk //...  2.06 us
    pallas_call x1, Pallas kernels, per_device(): pl.pallas_call(lon_kernel, out_shape=jax.ShapeDtypeStruct((lats, variable...  2.05 us
    pallas_call x1, Pallas kernels, per_device(): pl.pallas_call(lat_kernel, out_shape=jax.ShapeDtypeStruct((nlat, width),...  1.45 us
    unnamed x3, local copies, waits for them, and re-layouts  1.39 us
  transfers between devices with their start and end apart: 2, of which 1 were waited for; matrix products, arithmetic and copies ran while one was open for 3% of the time, Pallas kernels for 4%

profile of v5, /device:TPU:1, one launch (start us, length us, event | category | flops | bytes accessed | tf_op | source)
XLA Modules:
  0.0 53.1 jit_solution(7598898337294090126)
XLA Ops:
  0.0 0.0 copy-start
  0.0 3.2 %collective-permute-start = (bf16[4,1,64,2048]{3,2,1,0:T(8,128)(2,1)}, bf16[4,1,64,2048]{3,2,1,0:T(8,128)(2,1)S(1)}, u32[]{:S(2)}, u32[]{:S(2)}) collective-permute-start(bf16[4,1,64,2048]{3,2,1,0:T(8,128)(2,1)} %own.1), channel_id=1, source_target_pairs={{0,1},{1,0},{2,3},{3,2},{4,5},{5,4},{6,7},{7,6},{8,9},{9,8},{10,11... | collective-permute-start | bytes 3145736 | tf_op jit(solution)/shard_map/ppermute | solution.py:162
  3.2 3.1 %collective-permute-start.1 = (bf16[4,1,64,2048]{3,2,1,0:T(8,128)(2,1)}, bf16[4,1,64,2048]{3,2,1,0:T(8,128)(2,1)S(1)}, u32[]{:S(2)}, u32[]{:S(2)}) collective-permute-start(bf16[4,1,64,2048]{3,2,1,0:T(8,128)(2,1)} %own.1), channel_id=1, source_target_pairs={{1,2},{2,1},{5,6},{6,5},{9,10},{10,9},{13,14},{14,13},{17,18},{18,... | collective-permute-start | bytes 3145736 | tf_op jit(solution)/shard_map/ppermute | solution.py:163
  6.4 1.4 %copy.8.coef_hbm = f32[4,4,3]{2,1,0:T(4,128)} copy(f32[4,4,3]{1,0,2:T(4,128)} %param.8) | data formatting | bytes 384 | tf_op args[1]
  7.7 2.1 %operators.1 = (bf16[8,1024,256]{2,1,0:T(8,128)(2,1)S(1)}, bf16[1024,256]{1,0:T(8,128)(2,1)S(1)}, f32[16,128]{1,0:T(8,128)S(1)}) custom-call(s32[16]{0:T(128)} %band_hbm.1, s32[5]{0:T(128)} %lat_offs_hbm.1, s32[5]{0:T(128)} %lon_offs_hbm.1, f32[4,4,3]{2,1,0:T(4,128)} %copy.8.coef_hbm, bf16[8,5,128,128]{3,2,1,0:T(8,128)(2,1)} %table_hbm.1, ...), custom_call_target="tpu_custom_call" | custom-call | tf_op jit(solution)/shard_map/operators/pallas_call | solution.py:165
  9.8 0.0 collective-permute-done.chip
  9.8 11.2 %collective-permute-done.1.cross = bf16[4,1,64,2048]{3,2,1,0:T(8,128)(2,1)S(1)} collective-permute-done((bf16[4,1,64,2048]{3,2,1,0:T(8,128)(2,1)}, bf16[4,1,64,2048]{3,2,1,0:T(8,128)(2,1)S(1)}, u32[]{:S(2)}, u32[]{:S(2)}) %collective-permute-start.1) | collective-permute-done | bytes 1048608 | tf_op jit(solution)/shard_map/ppermute | solution.py:163
  21.1 0.0 copy-done
  21.1 1.5 %latitude.1 = bf16[2048,256]{1,0:T(8,128)(2,1)S(1)} custom-call(bf16[4,1,64,2048]{3,2,1,0:T(8,128)(2,1)S(1)} %copy-done, bf16[4,1,64,2048]{3,2,1,0:T(8,128)(2,1)S(1)} %collective-permute-done.chip, bf16[4,1,64,2048]{3,2,1,0:T(8,128)(2,1)S(1)} %collective-permute-done.1.cross, f32[16,128]{1,0:T(8,128)S(1)} %get-tuple-element.8.coef, ...), custom_call_target="tpu_custom_call" | custom-call | tf_op jit(solution)/shard_map/latitude/pallas_call | solution.py:199
  22.5 28.5 %all_to_all.9.data = bf16[64,32,256]{2,1,0:T(8,128)(2,1)S(1)} all-to-all(bf16[64,32,256]{2,1,0:T(8,128)(2,1)S(1)} %bitcast.2), channel_id=1, replica_groups=mesh['pencil'=64,'lev'=4] {'pencil'}, dimensions={0} | all-to-all | bytes 2097152 | tf_op jit(solution)/shard_map/all_to_all | solution.py:208
  51.0 2.1 %longitude.1 = f32[32,4,32,1,128]{4,3,2,1,0:T(1,128)} custom-call(bf16[64,32,256]{2,1,0:T(8,128)(2,1)S(1)} %all_to_all.9.data, bf16[1024,256]{1,0:T(8,128)(2,1)S(1)} %get-tuple-element.10.weights), custom_call_target="tpu_custom_call" | custom-call | tf_op jit(solution)/shard_map/longitude/pallas_call | solution.py:209
Async XLA Ops:
  0.0 21.1 %copy-start = (bf16[4,1,64,2048]{3,2,1,0:T(8,128)(2,1)S(1)}, bf16[4,1,64,2048]{3,2,1,0:T(8,128)(2,1)}, u32[]{:S(2)}) copy-start(bf16[4,1,64,2048]{3,2,1,0:T(8,128)(2,1)} %own.1) | copy-start | bytes 3145732
  0.0 9.8 %collective-permute-start = (bf16[4,1,64,2048]{3,2,1,0:T(8,128)(2,1)}, bf16[4,1,64,2048]{3,2,1,0:T(8,128)(2,1)S(1)}, u32[]{:S(2)}, u32[]{:S(2)}) collective-permute-start(bf16[4,1,64,2048]{3,2,1,0:T(8,128)(2,1)} %own.1), channel_id=1, source_target_pairs={{0,1},{1,0},{2,3},{3,2},{4,5},{5,4},{6,7},{7,6},{8,9},{9,8},{10,11... | collective-permute-start | bytes 3145736 | tf_op jit(solution)/shard_map/ppermute | solution.py:162
  3.2 17.8 %collective-permute-start.1 = (bf16[4,1,64,2048]{3,2,1,0:T(8,128)(2,1)}, bf16[4,1,64,2048]{3,2,1,0:T(8,128)(2,1)S(1)}, u32[]{:S(2)}, u32[]{:S(2)}) collective-permute-start(bf16[4,1,64,2048]{3,2,1,0:T(8,128)(2,1)} %own.1), channel_id=1, source_target_pairs={{1,2},{2,1},{5,6},{6,5},{9,10},{10,9},{13,14},{14,13},{17,18},{18,... | collective-permute-start | bytes 3145736 | tf_op jit(solution)/shard_map/ppermute | solution.py:163

commit v6 on v5

--- a/solution.py
+++ b/solution.py
@@ -69,7 +69,7 @@
     rows_of[:, (REACH + nblk) * BLK :] = zeros
     done = 0
     for pair in range(nblk // 2):
-        ready = min(nblk, 2 * pair + SPAN - REACH)
+        ready = nblk
         for t in range(done, ready):
             cols = slice(t * BLK, (t + 1) * BLK)
             for v in range(variables):
@@ -89,7 +89,7 @@
             weights[pair],
             preferred_element_type=jnp.float32,
         )
-        out[2 * pair * BLK : 2 * (pair + 1) * BLK, :] = total.T.astype(out.dtype)
+        out[2 * pair * BLK : 2 * (pair + 1) * BLK, :] = total.astype(out.dtype).T
 
 
 def lon_kernel(data, weights, out, rows_of, stage, sem):

time: 53.3 us -> 53.2 us (level)
  no operation moved by 1% of the time
where the time goes in v6:
time: 53.2 us; the launch traced here: 53 us
  blocking collectives  28.5 us (54%)
  waiting for transfers between devices  11.2 us (21%)
  starting transfers between devices  6.34 us (12%)
  Pallas kernels  5.51 us (10%)
  local copies, waits for them, and re-layouts  1.39 us (3%)
    all_to_all x1, blocking collectives, per_device(): lax.all_to_all(filtered, 'pencil', split_axis=0, concat_axis=0, tiled=True)  28.5 us
    ppermute x1, waiting for transfers between devices, per_device(): cross = lax.ppermute(increment, 'lev', cross_pairs)  11.2 us
    ppermute x1, starting transfers between devices, per_device(): chip = lax.ppermute(increment, 'lev', chip_pairs)  3.24 us
    ppermute x1, starting transfers between devices, per_device(): cross = lax.ppermute(increment, 'lev', cross_pairs)  3.1 us
    pallas_call x1, Pallas kernels, per_device(): pl.pallas_call(operator_kernel, out_shape=(jax.ShapeDtypeStruct((nblk //...  2.06 us
    pallas_call x1, Pallas kernels, per_device(): pl.pallas_call(lon_kernel, out_shape=jax.ShapeDtypeStruct((lats, variable...  2.05 us
    pallas_call x1, Pallas kernels, per_device(): pl.pallas_call(lat_kernel, out_shape=jax.ShapeDtypeStruct((nlat, width),...  1.4 us
    unnamed x3, local copies, waits for them, and re-layouts  1.39 us
  transfers between devices with their start and end apart: 2, of which 1 were waited for; matrix products, arithmetic and copies ran while one was open for 3% of the time, Pallas kernels for 4%

profile of v6, /device:TPU:1, one launch (start us, length us, event | category | flops | bytes accessed | tf_op | source)
XLA Modules:
  0.0 53.0 jit_solution(17225780577454321990)
XLA Ops:
  0.0 0.0 copy-start
  0.0 3.2 %collective-permute-start = (bf16[4,1,64,2048]{3,2,1,0:T(8,128)(2,1)}, bf16[4,1,64,2048]{3,2,1,0:T(8,128)(2,1)S(1)}, u32[]{:S(2)}, u32[]{:S(2)}) collective-permute-start(bf16[4,1,64,2048]{3,2,1,0:T(8,128)(2,1)} %own.1), channel_id=1, source_target_pairs={{0,1},{1,0},{2,3},{3,2},{4,5},{5,4},{6,7},{7,6},{8,9},{9,8},{10,11... | collective-permute-start | bytes 3145736 | tf_op jit(solution)/shard_map/ppermute | solution.py:162
  3.2 3.1 %collective-permute-start.1 = (bf16[4,1,64,2048]{3,2,1,0:T(8,128)(2,1)}, bf16[4,1,64,2048]{3,2,1,0:T(8,128)(2,1)S(1)}, u32[]{:S(2)}, u32[]{:S(2)}) collective-permute-start(bf16[4,1,64,2048]{3,2,1,0:T(8,128)(2,1)} %own.1), channel_id=1, source_target_pairs={{1,2},{2,1},{5,6},{6,5},{9,10},{10,9},{13,14},{14,13},{17,18},{18,... | collective-permute-start | bytes 3145736 | tf_op jit(solution)/shard_map/ppermute | solution.py:163
  6.4 1.4 %copy.8.coef_hbm = f32[4,4,3]{2,1,0:T(4,128)} copy(f32[4,4,3]{1,0,2:T(4,128)} %param.8) | data formatting | bytes 384 | tf_op args[1]
  7.7 2.1 %operators.1 = (bf16[8,1024,256]{2,1,0:T(8,128)(2,1)S(1)}, bf16[1024,256]{1,0:T(8,128)(2,1)S(1)}, f32[16,128]{1,0:T(8,128)S(1)}) custom-call(s32[16]{0:T(128)} %band_hbm.1, s32[5]{0:T(128)} %lat_offs_hbm.1, s32[5]{0:T(128)} %lon_offs_hbm.1, f32[4,4,3]{2,1,0:T(4,128)} %copy.8.coef_hbm, bf16[8,5,128,128]{3,2,1,0:T(8,128)(2,1)} %table_hbm.1, ...), custom_call_target="tpu_custom_call" | custom-call | tf_op jit(solution)/shard_map/operators/pallas_call | solution.py:165
  9.8 0.0 collective-permute-done.chip
  9.8 11.2 %collective-permute-done.1.cross = bf16[4,1,64,2048]{3,2,1,0:T(8,128)(2,1)S(1)} collective-permute-done((bf16[4,1,64,2048]{3,2,1,0:T(8,128)(2,1)}, bf16[4,1,64,2048]{3,2,1,0:T(8,128)(2,1)S(1)}, u32[]{:S(2)}, u32[]{:S(2)}) %collective-permute-start.1) | collective-permute-done | bytes 1048608 | tf_op jit(solution)/shard_map/ppermute | solution.py:163
  21.1 0.0 copy-done
  21.1 1.4 %latitude.1 = bf16[2048,256]{1,0:T(8,128)(2,1)S(1)} custom-call(bf16[4,1,64,2048]{3,2,1,0:T(8,128)(2,1)S(1)} %copy-done, bf16[4,1,64,2048]{3,2,1,0:T(8,128)(2,1)S(1)} %collective-permute-done.chip, bf16[4,1,64,2048]{3,2,1,0:T(8,128)(2,1)S(1)} %collective-permute-done.1.cross, f32[16,128]{1,0:T(8,128)S(1)} %get-tuple-element.8.coef, ...), custom_call_target="tpu_custom_call" | custom-call | tf_op jit(solution)/shard_map/latitude/pallas_call | solution.py:199
  22.5 28.5 %all_to_all.9.data = bf16[64,32,256]{2,1,0:T(8,128)(2,1)S(1)} all-to-all(bf16[64,32,256]{2,1,0:T(8,128)(2,1)S(1)} %bitcast.2), channel_id=1, replica_groups=mesh['pencil'=64,'lev'=4] {'pencil'}, dimensions={0} | all-to-all | bytes 2097152 | tf_op jit(solution)/shard_map/all_to_all | solution.py:208
  51.0 2.0 %longitude.1 = f32[32,4,32,1,128]{4,3,2,1,0:T(1,128)} custom-call(bf16[64,32,256]{2,1,0:T(8,128)(2,1)S(1)} %all_to_all.9.data, bf16[1024,256]{1,0:T(8,128)(2,1)S(1)} %get-tuple-element.10.weights), custom_call_target="tpu_custom_call" | custom-call | tf_op jit(solution)/shard_map/longitude/pallas_call | solution.py:209
Async XLA Ops:
  0.0 21.1 %copy-start = (bf16[4,1,64,2048]{3,2,1,0:T(8,128)(2,1)S(1)}, bf16[4,1,64,2048]{3,2,1,0:T(8,128)(2,1)}, u32[]{:S(2)}) copy-start(bf16[4,1,64,2048]{3,2,1,0:T(8,128)(2,1)} %own.1) | copy-start | bytes 3145732
  0.0 9.8 %collective-permute-start = (bf16[4,1,64,2048]{3,2,1,0:T(8,128)(2,1)}, bf16[4,1,64,2048]{3,2,1,0:T(8,128)(2,1)S(1)}, u32[]{:S(2)}, u32[]{:S(2)}) collective-permute-start(bf16[4,1,64,2048]{3,2,1,0:T(8,128)(2,1)} %own.1), channel_id=1, source_target_pairs={{0,1},{1,0},{2,3},{3,2},{4,5},{5,4},{6,7},{7,6},{8,9},{9,8},{10,11... | collective-permute-start | bytes 3145736 | tf_op jit(solution)/shard_map/ppermute | solution.py:162
  3.2 17.8 %collective-permute-start.1 = (bf16[4,1,64,2048]{3,2,1,0:T(8,128)(2,1)}, bf16[4,1,64,2048]{3,2,1,0:T(8,128)(2,1)S(1)}, u32[]{:S(2)}, u32[]{:S(2)}) collective-permute-start(bf16[4,1,64,2048]{3,2,1,0:T(8,128)(2,1)} %own.1), channel_id=1, source_target_pairs={{1,2},{2,1},{5,6},{6,5},{9,10},{10,9},{13,14},{14,13},{17,18},{18,... | collective-permute-start | bytes 3145736 | tf_op jit(solution)/shard_map/ppermute | solution.py:163
